TPU v7x, 32 devices: a whole 2x2x4 slice. The times are simulated.
32 devices in a mesh: seq: 4 (over z), fsdp: 8 (over y, x, core).
Axes of the slice: x: 2, y: 2, z: 4, core: 2. Of those that a mesh axis runs over, the one named last changes fastest.
Arguments:
- hidden_in: bfloat16 [16, 1024, 1024], P('fsdp', 'seq'), may hold values from -6 to 6
- document_labels: int32 [16, 1024], P('fsdp', 'seq'), may hold values from 0 to 2, never falling along the last dimension, each value on 1 to 512 neighbouring positions
- cotangent: bfloat16 [16, 1024, 1024], P('fsdp', 'seq'), may hold values from -6 to 6
- ln_gain: bfloat16 [1024], P(('seq', 'fsdp')), may hold values from 0.5 to 1.5
- ln_bias: bfloat16 [1024], P(('seq', 'fsdp')), may hold values from -1 to 1
- qkv_weight: bfloat16 [1024, 3072], P(('seq', 'fsdp')), may hold values from -0.1875 to 0.1875
- qkv_bias: bfloat16 [3072], P(('seq', 'fsdp')), may hold values from -1 to 1
- out_weight: bfloat16 [1024, 1024], P(('seq', 'fsdp')), may hold values from -1.5 to 1.5
- out_bias: bfloat16 [1024], P(('seq', 'fsdp')), may hold values from -1 to 1
- fc_in_weight: bfloat16 [1024, 4096], P(('seq', 'fsdp')), may hold values from -0.1875 to 0.1875
- fc_in_bias: bfloat16 [4096], P(('seq', 'fsdp')), may hold values from -1 to 1
- fc_out_weight: bfloat16 [4096, 1024], P(('seq', 'fsdp')), may hold values from -0.09375 to 0.09375
- fc_out_bias: bfloat16 [1024], P(('seq', 'fsdp')), may hold values from -1 to 1
Outputs:
- output: bfloat16 [16, 1024, 1024], P('fsdp', 'seq')
- input_grad: bfloat16 [16, 1024, 1024], P('fsdp', 'seq')
- ln_gain_grad: float32 [1024], P(('seq', 'fsdp'))
- ln_bias_grad: float32 [1024], P(('seq', 'fsdp'))
- qkv_weight_grad: float32 [1024, 3072], P(('seq', 'fsdp'))
- qkv_bias_grad: float32 [3072], P(('seq', 'fsdp'))
- out_weight_grad: float32 [1024, 1024], P(('seq', 'fsdp'))
- out_bias_grad: float32 [1024], P(('seq', 'fsdp'))
- fc_in_weight_grad: float32 [1024, 4096], P(('seq', 'fsdp'))
- fc_in_bias_grad: float32 [4096], P(('seq', 'fsdp'))
- fc_out_weight_grad: float32 [4096, 1024], P(('seq', 'fsdp'))
- fc_out_bias_grad: float32 [1024], P(('seq', 'fsdp'))
Inputs may be any that keep to these rules, and one draw needn't show every extreme that they name: `document_labels`: along each sequence the numbers never fall; every document (a run of equal numbers) has 1 to 512 tokens, and one has exactly 512.
All inputs are finite; a program needn't handle non-finite values.
Results may differ from a plain program's by a relative error of at most 0.009.
Values may be sent and summed in bfloat16 or wider, within the bound.
No kernel may reach another device: no remote copies, remote signals or barrier semaphores. Data moves between devices by JAX's collectives and lax.ppermute only.
A program may use at most 256 MiB of HBM per device.

v0:
```python
from functools import partial
import math

import jax
import jax.numpy as jnp
from jax import lax
from jax.sharding import PartitionSpec as P

D = 1024
H = 16
HD = 64
ROT = 16


def rotate(values, cosine, sine_part):
    half_rot = ROT // 2
    first_part = values[..., :half_rot]
    second_part = values[..., half_rot:ROT]
    return jnp.concatenate(
        [
            first_part * cosine - second_part * sine_part,
            second_part * cosine + first_part * sine_part,
            values[..., ROT:],
        ],
        axis=-1,
    )


def position_angles(segments):
    length = segments.shape[0]
    places = jnp.arange(length, dtype=jnp.int32)
    boundary = jnp.concatenate([jnp.ones((1,), dtype=jnp.bool_), segments[1:] != segments[:-1]])
    starts = lax.cummax(jnp.where(boundary, places, 0), axis=0)
    positions = (places - starts).astype(jnp.float32)
    inverse = 1.0 / 10000.0 ** (jnp.arange(0, ROT, 2, dtype=jnp.float32) / ROT)
    return positions[:, None] * inverse[None, :]


def make_mask(segments, first_row, block_rows):
    length = segments.shape[0]
    query_index = first_row + jnp.arange(block_rows, dtype=jnp.int32)
    key_index = jnp.arange(length, dtype=jnp.int32)
    query_segments = lax.dynamic_slice_in_dim(segments, first_row, block_rows, 0)
    return (key_index[None, :] <= query_index[:, None]) & (
        query_segments[:, None] == segments[None, :]
    )


def outer_product(left, right):
    return lax.dot_general(
        left, right, (((0,), (0,)), ((), ())), preferred_element_type=jnp.float32
    )


def times_transposed(left, right):
    return lax.dot_general(
        left, right, (((1,), (1,)), ((), ())), preferred_element_type=jnp.float32
    )


def local(
    hidden_in,
    document_labels,
    cotangent,
    ln_gain,
    ln_bias,
    qkv_weight,
    qkv_bias,
    out_weight,
    out_bias,
    fc_in_weight,
    fc_in_bias,
    fc_out_weight,
    fc_out_bias,
):
    gathered = (
        lax.all_gather(ln_gain, ("seq", "fsdp"), axis=0, tiled=True),
        lax.all_gather(ln_bias, ("seq", "fsdp"), axis=0, tiled=True),
        lax.all_gather(qkv_weight, ("seq", "fsdp"), axis=0, tiled=True),
        lax.all_gather(qkv_bias, ("seq", "fsdp"), axis=0, tiled=True),
        lax.all_gather(out_weight, ("seq", "fsdp"), axis=0, tiled=True),
        lax.all_gather(out_bias, ("seq", "fsdp"), axis=0, tiled=True),
        lax.all_gather(fc_in_weight, ("seq", "fsdp"), axis=0, tiled=True),
        lax.all_gather(fc_in_bias, ("seq", "fsdp"), axis=0, tiled=True),
        lax.all_gather(fc_out_weight, ("seq", "fsdp"), axis=0, tiled=True),
        lax.all_gather(fc_out_bias, ("seq", "fsdp"), axis=0, tiled=True),
    )
    norm_multiplier, norm_shift, w_qkv, b_qkv, w_out, b_out, w_in, b_in, w_fc, b_fc = gathered
    norm_multiplier = norm_multiplier.astype(jnp.float32)
    norm_shift = norm_shift.astype(jnp.float32)
    groups = lax.axis_size("seq")
    per_group = H // groups
    local_seqs = hidden_in.shape[0]
    tok_count = hidden_in.shape[1]
    row_count = local_seqs * tok_count
    tokens = hidden_in.reshape(row_count, D).astype(jnp.float32)
    average = jnp.mean(tokens, axis=-1, keepdims=True)
    centered = tokens - average
    spread = jnp.mean(centered * centered, axis=-1, keepdims=True)
    inv_std = lax.rsqrt(spread + 1e-05)
    rescaled_rows = centered * inv_std
    normed = (rescaled_rows * norm_multiplier + norm_shift).astype(jnp.bfloat16)
    projected = jnp.dot(normed, w_qkv, preferred_element_type=jnp.float32) + b_qkv.astype(
        jnp.float32
    )
    segments_all = lax.all_gather(document_labels, "seq", axis=1, tiled=True)
    angles_all = jax.vmap(position_angles)(segments_all)
    angles = lax.dynamic_slice_in_dim(
        angles_all, lax.axis_index("seq") * tok_count, tok_count, 1
    ).reshape(row_count, ROT // 2)
    cosine = jnp.cos(angles)[:, None, None, :]
    sine_part = jnp.sin(angles)[:, None, None, :]
    head_parts = projected.reshape(row_count, H, 3, HD)
    turned = jnp.concatenate(
        [rotate(head_parts[:, :, :2], cosine, sine_part), head_parts[:, :, 2:]], axis=2
    ).astype(jnp.bfloat16)
    outgoing = turned.reshape(local_seqs, tok_count, groups, per_group * 3 * HD)
    arrived = lax.all_to_all(outgoing, "seq", split_axis=2, concat_axis=1, tiled=True)
    length = arrived.shape[1]
    local_heads = arrived.reshape(local_seqs, length, per_group, 3, HD)
    queries_seq = local_heads[:, :, :, 0]
    keys_seq = local_heads[:, :, :, 1]
    values_seq = local_heads[:, :, :, 2]
    block_rows = min(512, length)
    block_count = length // block_rows
    scale_factor = 1.0 / math.sqrt(HD)

    def attend_forward(inputs):
        query_all, key_everywhere, value_all, segments = inputs

        def forward_step(running, block_index):
            first_row = block_index * block_rows
            query_rows = lax.dynamic_slice_in_dim(query_all, first_row, block_rows, 0)
            allowed = make_mask(segments, first_row, block_rows)
            raw_scores = (
                jnp.einsum(
                    "qhd,khd->hqk", query_rows, key_everywhere, preferred_element_type=jnp.float32
                )
                * scale_factor
            )
            raw_scores = jnp.where(allowed[None], raw_scores, -1e30)
            row_max = jnp.max(raw_scores, axis=-1, keepdims=True)
            unscaled = jnp.exp(raw_scores - row_max)
            row_total = jnp.sum(unscaled, axis=-1, keepdims=True)
            probabilities = (unscaled / row_total).astype(jnp.bfloat16)
            context_rows = jnp.einsum(
                "hqk,khd->qhd", probabilities, value_all, preferred_element_type=jnp.float32
            )
            log_total = (row_max + jnp.log(row_total))[..., 0]
            return (running, (context_rows, log_total))

        _, (context_blocks, log_blocks) = lax.scan(
            forward_step, None, jnp.arange(block_count, dtype=jnp.int32)
        )
        return (context_blocks.reshape(length, per_group * HD).astype(jnp.bfloat16), log_blocks)

    context_seq, log_totals = lax.map(
        attend_forward, (queries_seq, keys_seq, values_seq, segments_all)
    )
    context_heads = context_seq.reshape(local_seqs, length, 1, per_group * HD)
    returned = lax.all_to_all(context_heads, "seq", split_axis=1, concat_axis=2, tiled=True)
    context = returned.reshape(row_count, D)
    attn_out = jnp.dot(context, w_out, preferred_element_type=jnp.float32) + b_out.astype(
        jnp.float32
    )
    hidden_pre = jnp.dot(normed, w_in, preferred_element_type=jnp.float32) + b_in.astype(
        jnp.float32
    )
    activated = jax.nn.gelu(hidden_pre, approximate=False).astype(jnp.bfloat16)
    mlp_out = jnp.dot(activated, w_fc, preferred_element_type=jnp.float32) + b_fc.astype(
        jnp.float32
    )
    output = (tokens + attn_out + mlp_out).astype(jnp.bfloat16).reshape(local_seqs, tok_count, D)
    grad_out = cotangent.reshape(row_count, D)
    grad_wide = grad_out.astype(jnp.float32)
    out_bias_grad = jnp.sum(grad_wide, axis=0)
    fc_out_bias_grad = jnp.sum(grad_wide, axis=0)
    out_weight_grad = outer_product(context, grad_out)
    fc_out_weight_grad = outer_product(activated, grad_out)
    act_grad = times_transposed(grad_out, w_fc)
    _, gelu_back = jax.vjp(partial(jax.nn.gelu, approximate=False), hidden_pre)
    hidden_grad = gelu_back(act_grad)[0].astype(jnp.bfloat16)
    fc_in_weight_grad = outer_product(normed, hidden_grad)
    fc_in_bias_grad = jnp.sum(hidden_grad.astype(jnp.float32), axis=0)
    context_grad = times_transposed(grad_out, w_out).astype(jnp.bfloat16)
    grad_outgoing = context_grad.reshape(local_seqs, tok_count, groups, per_group * HD)
    head_grad_seq = lax.all_to_all(
        grad_outgoing, "seq", split_axis=2, concat_axis=1, tiled=True
    ).reshape(local_seqs, length, per_group, HD)

    def attend_backward(inputs):
        query_all, key_everywhere, value_all, segments, head_grad, log_blocks = inputs

        def backward_step(running, block_index):
            key_acc, value_accumulator = running
            first_row = block_index * block_rows
            query_rows = lax.dynamic_slice_in_dim(query_all, first_row, block_rows, 0)
            grad_rows = lax.dynamic_slice_in_dim(head_grad, first_row, block_rows, 0)
            log_rows = log_blocks[block_index]
            allowed = make_mask(segments, first_row, block_rows)
            raw_scores = (
                jnp.einsum(
                    "qhd,khd->hqk", query_rows, key_everywhere, preferred_element_type=jnp.float32
                )
                * scale_factor
            )
            raw_scores = jnp.where(allowed[None], raw_scores, -1e30)
            probabilities = jnp.where(allowed[None], jnp.exp(raw_scores - log_rows[..., None]), 0.0)
            value_accumulator = value_accumulator + jnp.einsum(
                "hqk,qhd->khd",
                probabilities.astype(jnp.bfloat16),
                grad_rows,
                preferred_element_type=jnp.float32,
            )
            prob_grad = jnp.einsum(
                "qhd,khd->hqk", grad_rows, value_all, preferred_element_type=jnp.float32
            )
            inner_total = jnp.sum(probabilities * prob_grad, axis=-1, keepdims=True)
            score_grad = (probabilities * (prob_grad - inner_total)).astype(jnp.bfloat16)
            query_grad = (
                jnp.einsum(
                    "hqk,khd->qhd", score_grad, key_everywhere, preferred_element_type=jnp.float32
                )
                * scale_factor
            )
            key_acc = (
                key_acc
                + jnp.einsum(
                    "hqk,qhd->khd", score_grad, query_rows, preferred_element_type=jnp.float32
                )
                * scale_factor
            )
            return ((key_acc, value_accumulator), query_grad)

        empty_grad = jnp.zeros((length, per_group, HD), jnp.float32)
        (key_grad, value_grad), query_blocks = lax.scan(
            backward_step, (empty_grad, empty_grad), jnp.arange(block_count, dtype=jnp.int32)
        )
        query_grad = query_blocks.reshape(length, per_group, HD)
        return jnp.stack([query_grad, key_grad, value_grad], axis=2).astype(jnp.bfloat16)

    stacked = lax.map(
        attend_backward,
        (queries_seq, keys_seq, values_seq, segments_all, head_grad_seq, log_totals),
    )
    returned_grad = lax.all_to_all(
        stacked.reshape(local_seqs, length, 1, per_group * 3 * HD),
        "seq",
        split_axis=1,
        concat_axis=2,
        tiled=True,
    )
    back_heads = returned_grad.reshape(row_count, H, 3, HD).astype(jnp.float32)
    unturned = jnp.concatenate(
        [rotate(back_heads[:, :, :2], cosine, -sine_part), back_heads[:, :, 2:]], axis=2
    )
    projected_grad = unturned.reshape(row_count, 3 * D).astype(jnp.bfloat16)
    qkv_weight_grad = outer_product(normed, projected_grad)
    qkv_bias_grad = jnp.sum(projected_grad.astype(jnp.float32), axis=0)
    normalized_gradient = times_transposed(projected_grad, w_qkv) + times_transposed(
        hidden_grad, w_in
    )
    ln_gain_grad = jnp.sum(normalized_gradient * rescaled_rows, axis=0)
    ln_bias_grad = jnp.sum(normalized_gradient, axis=0)
    standardized_gradient = normalized_gradient * norm_multiplier
    norm_back = (
        standardized_gradient
        - jnp.mean(standardized_gradient, axis=-1, keepdims=True)
        - rescaled_rows * jnp.mean(standardized_gradient * rescaled_rows, axis=-1, keepdims=True)
    ) * inv_std
    input_grad = (grad_wide + norm_back).astype(jnp.bfloat16).reshape(local_seqs, tok_count, D)
    summed = (
        lax.psum_scatter(ln_gain_grad, ("seq", "fsdp"), scatter_dimension=0, tiled=True),
        lax.psum_scatter(ln_bias_grad, ("seq", "fsdp"), scatter_dimension=0, tiled=True),
        lax.psum_scatter(qkv_weight_grad, ("seq", "fsdp"), scatter_dimension=0, tiled=True),
        lax.psum_scatter(qkv_bias_grad, ("seq", "fsdp"), scatter_dimension=0, tiled=True),
        lax.psum_scatter(out_weight_grad, ("seq", "fsdp"), scatter_dimension=0, tiled=True),
        lax.psum_scatter(out_bias_grad, ("seq", "fsdp"), scatter_dimension=0, tiled=True),
        lax.psum_scatter(fc_in_weight_grad, ("seq", "fsdp"), scatter_dimension=0, tiled=True),
        lax.psum_scatter(fc_in_bias_grad, ("seq", "fsdp"), scatter_dimension=0, tiled=True),
        lax.psum_scatter(fc_out_weight_grad, ("seq", "fsdp"), scatter_dimension=0, tiled=True),
        lax.psum_scatter(fc_out_bias_grad, ("seq", "fsdp"), scatter_dimension=0, tiled=True),
    )
    return (
        output,
        input_grad,
        summed[0],
        summed[1],
        summed[2],
        summed[3],
        summed[4],
        summed[5],
        summed[6],
        summed[7],
        summed[8],
        summed[9],
    )


def solution(mesh):
    placed = (
        P("fsdp", "seq", None),
        P("fsdp", "seq"),
        P("fsdp", "seq", None),
        P(("seq", "fsdp")),
        P(("seq", "fsdp")),
        P(("seq", "fsdp"), None),
        P(("seq", "fsdp")),
        P(("seq", "fsdp"), None),
        P(("seq", "fsdp")),
        P(("seq", "fsdp"), None),
        P(("seq", "fsdp")),
        P(("seq", "fsdp"), None),
        P(("seq", "fsdp")),
    )
    return jax.shard_map(
        local,
        mesh=mesh,
        in_specs=placed,
        out_specs=(
            P("fsdp", "seq", None),
            P("fsdp", "seq", None),
            P(("seq", "fsdp")),
            P(("seq", "fsdp")),
            P(("seq", "fsdp"), None),
            P(("seq", "fsdp")),
            P(("seq", "fsdp"), None),
            P(("seq", "fsdp")),
            P(("seq", "fsdp"), None),
            P(("seq", "fsdp")),
            P(("seq", "fsdp"), None),
            P(("seq", "fsdp")),
        ),
        check_vma=False,
    )
```

profile of v0, /device:TPU:1, one launch (start us, length us, event | category | flops | bytes accessed | tf_op | source)
XLA Modules:
  0.0 1090.7 jit_solution(5082367218466771486)
XLA Ops:
  13.6 42.0 %all-reduce.12 = (bf16[1024]{0:T(1024)(128)(2,1)S(1)}, bf16[1024]{0:T(1024)(128)(2,1)S(1)}, bf16[3072]{0:T(1024)(128)(2,1)S(1)}, bf16[1024]{0:T(1024)(128)(2,1)}, bf16[1024]{0:T(1024)(128)(2,1)}) all-reduce(bf16[1024]{0:T(1024)(128)(2,1)S(1)} %dynamic-update-slice.1, ...), channel_id=1, replica_groups=mesh['seq'=4,'fsdp'=8] {'seq','fsdp'}, use_global_device_ids=true, to_apply=%add.2 | all-reduce | flops 7168 | bytes 28672
  59.3 9.8 all_gather.37
  72.3 10.6 all-gather.6.cloned.1.call-done
  82.9 8.1 convolution_add_fusion
  91.0 6.6 copy.50
  105.9 3.7 all-to-all-start
  110.2 63.6 %all-gather.8.cloned.1.call-done = bf16[1024,1024]{1,0:T(8,128)(2,1)} async-done(((bf16[32,1024]{1,0:T(8,128)(2,1)}), bf16[1024,1024]{1,0:T(8,128)(2,1)}) %all-gather.8.cloned.1.call-update) | async-done | bytes 2097168 | tf_op jit(solution)/shard_map/all_gather | solution.py:81
  173.8 4.2 convolution_convert_fusion
  183.0 5.2 all-to-all-done
  188.1 4.4 all-to-all-start.2
  192.6 4.1 copy.51
  196.6 4.7 reshape.387
  203.1 44.6 %while.50 = (s32[]{:T(128)}, bf16[2,1024,256]{1,2,0:T(8,128)(2,1)}, f32[2,2,4,512]{3,2,1,0:T(4,128)S(1)}, bf16[2,1024,4,64]{1,3,2,0:T(8,128)(2,1)}, s32[2,1024]{...) while((s32[]{:T(128)}, bf16[2,1024,256]{1,2,0:T(8,128)(2,1)}, ...), condition=%wide.region_9.10_spmd, body=%wide.region_4.9_spmd.sunk | while | flops 563608064 | bytes 43899404 | solution.py:157
  205.5 17.9 %while.53 = (s32[]{:T(128)}, bf16[2,512,4,64]{1,3,2,0:T(8,128)(2,1)S(1)}, f32[2,4,512]{2,1,0:T(4,128)S(1)}, s32[2]{0:T(128)S(1)}, s32[1024]{0:T(1024)S(1)}, /*in...) while((s32[]{:T(128)}, ...), condition=%wide.region_8.8_spmd, body=%wide.region_5.7_spmd.sunk | while | flops 563608064 | bytes 29178060 | solution.py:152
  227.8 17.9 %while.53 = (s32[]{:T(128)}, bf16[2,512,4,64]{1,3,2,0:T(8,128)(2,1)S(1)}, f32[2,4,512]{2,1,0:T(4,128)S(1)}, s32[2]{0:T(128)S(1)}, s32[1024]{0:T(1024)S(1)}, /*in...) while((s32[]{:T(128)}, ...), condition=%wide.region_8.8_spmd, body=%wide.region_5.7_spmd.sunk | while | flops 563608064 | bytes 29178060 | solution.py:152
  247.6 3.7 copy.52
  251.4 4.5 all-to-all-start.1
  259.1 28.3 %all-to-all-done.1 = bf16[2,1024,1,256]{3,0,2,1:T(2,128)(2,1)S(1)} async-done(((bf16[2,1024,1,256]{3,0,2,1:T(2,128)(2,1)}), bf16[2,1024,1,256]{3,0,2,1:T(2,128)(2,1)S(1)}, u32[]{:S(2)}, u32[]{:S(2)}) %all-to-all-start.1) | async-done | bytes 1048608 | tf_op jit(solution)/shard_map/all_to_all | solution.py:161
  292.8 130.3 %while.52 = (s32[]{:T(128)}, bf16[2,1024,4,3,64]{1,4,3,2,0:T(8,128)(2,1)}, bf16[2,1024,4,64]{1,3,2,0:T(8,128)(2,1)}, bf16[2,1024,4,64]{1,3,2,0:T(8,128)(2,1)}, f...) while((s32[]{:T(128)}, ...), condition=%wide.region_14.15_spmd, body=%wide.region_10.14_spmd.sunk | while | flops 1368259072 | bytes 199326544 | solution.py:242
  296.9 58.0 %while.54 = (s32[]{:T(128)}, f32[1024,4,64]{0,2,1:T(8,128)S(1)}, f32[1024,4,64]{0,2,1:T(8,128)S(1)}, bf16[2,512,4,64]{1,3,2,0:T(8,128)(2,1)}, s32[2]{0:T(128)S(1...) while((s32[]{:T(128)}, f32[1024,4,64]{0,2,1:T(8,128)S(1)}, ...), condition=%wide.region_13.13_spmd.clone, body=%wide.region_11.12_spmd.clone.sunk | while | flops 1366161920 | bytes 186702352 | solution.py:236
  298.1 4.6 fusion.132
  305.3 7.3 multiply_reduce_fusion.3
  326.9 4.6 fusion.132
  334.0 7.3 multiply_reduce_fusion.3
  345.9 3.5 fusion.134
  361.9 57.6 %while.54 = (s32[]{:T(128)}, f32[1024,4,64]{0,2,1:T(8,128)S(1)}, f32[1024,4,64]{0,2,1:T(8,128)S(1)}, bf16[2,512,4,64]{1,3,2,0:T(8,128)(2,1)}, s32[2]{0:T(128)S(1...) while((s32[]{:T(128)}, f32[1024,4,64]{0,2,1:T(8,128)S(1)}, ...), condition=%wide.region_13.13_spmd.clone, body=%wide.region_11.12_spmd.clone.sunk | while | flops 1366161920 | bytes 186702352 | solution.py:236
  363.2 4.6 fusion.132
  370.3 7.3 multiply_reduce_fusion.3
  392.0 4.6 fusion.132
  399.2 7.3 multiply_reduce_fusion.3
  423.1 8.9 copy.57
  432.0 4.6 all-to-all-start.3
  437.2 75.5 %all-to-all-done.3 = bf16[2,1024,1,768]{3,0,2,1:T(2,128)(2,1)} async-done(((bf16[2,1024,1,768]{3,0,2,1:T(2,128)(2,1)}), bf16[2,1024,1,768]{3,0,2,1:T(2,128)(2,1)}, u32[]{:S(2)}, u32[]{:S(2)}) %all-to-all-start.3) | async-done | bytes 3145760 | tf_op jit(solution)/shard_map/all_to_all | solution.py:246
  518.2 10.3 copy.59
  528.5 9.0 reshape.397
  545.7 6.3 fusion.68
  552.7 39.5 %all-gather = bf16[32,1,128]{2,1,0:T(2,128)(2,1)S(1)} all-gather(bf16[1,1,128]{2,1,0:T(2,128)(2,1)S(1)} %bitcast.266), channel_id=1, replica_groups=mesh['seq'=4,'fsdp'=8] {'seq','fsdp'}, dimensions={0}, use_global_device_ids=true | all-gather | bytes 8448 | tf_op jit(solution)/shard_map/all_gather | solution.py:84
  592.2 10.9 fusion.65
  603.1 27.4 %convert_reduce_fusion = (f32[4096]{0:T(1024)S(1)}, bf16[512,4096]{1,0:T(8,128)(2,1)S(1)}, f32[512,4096]{1,0:T(8,128)}) fusion(f32[512,4096]{1,0:T(8,128)} %fusion.65, f32[4096]{0:T(1024)S(1)} %bitcast.256, bf16[512,1024]{1,0:T(8,128)(2,1)S(1)} %bitcast.239, bf16[4096,1024]{1,0:T(8,128)(2,1)} %all-gather.12.cloned.1.call-done), kind=kOutput, calls=%fused_computation.61 | convolution fusion | flops 4452249600 | bytes 30441472 | tf_op jit(solution)/shard_map/dot_general | solution.py:56
  632.5 8.3 fusion.70
  640.9 8.2 multiply_convert_fusion.1
  651.2 8.3 fusion.71
  660.5 8.3 fusion.66
  668.8 8.4 fusion.67
  679.8 9.9 fusion.57
  689.7 41.5 %all-reduce.11 = (f32[1024]{0:T(1024)S(1)}, f32[1024]{0:T(1024)S(1)}, f32[3072]{0:T(1024)S(1)}, f32[1024]{0:T(1024)S(1)}, f32[4096]{0:T(1024)S(1)}) all-reduce(f32[1024]{0:T(1024)S(1)} %get-tuple-element.233, f32[1024]{0:T(1024)S(1)} %get-tuple-element.236, ...), channel_id=2, replica_groups=mesh['seq'=4,'fsdp'=8] {'seq','fsdp'}, use_global_device_ids=true, to_apply=%region_18.19.clone | all-reduce | flops 10240 | bytes 81920
  737.1 158.3 %reduce-scatter.9.cloned.1.call-done = f32[32,4096]{1,0:T(8,128)} async-done(((f32[1024,4096]{1,0:T(8,128)}), f32[32,4096]{1,0:T(8,128)}) %reduce-scatter.9.cloned.1.call-update) | async-done | bytes 524304 | tf_op jit(solution)/shard_map/reduce_scatter | solution.py:279
  895.3 187.7 %reduce-scatter.11.cloned.1.call-done = f32[128,1024]{1,0:T(8,128)} async-done(((f32[4096,1024]{1,0:T(8,128)}), f32[128,1024]{1,0:T(8,128)}) %reduce-scatter.11.cloned.1.call-update) | async-done | bytes 524304 | tf_op jit(solution)/shard_map/reduce_scatter | solution.py:281
  (348 shorter events, 175.5 us)
Async XLA Ops:
  7.2 75.7 %all-gather.6.cloned.1.call-start = ((), (), s32[]{:S(2)}) async-start(), calls=%async_computation.8 | async-start | bytes 6488064 | tf_op jit(solution)/shard_map/all_gather | solution.py:79
  7.9 165.9 %all-gather.8.cloned.1.call-start = ((), (), s32[]{:S(2)}) async-start(), calls=%async_computation.9 | async-start | bytes 2162688 | tf_op jit(solution)/shard_map/all_gather | solution.py:81
  8.7 583.5 %all-gather.10.cloned.1.call-start = ((), (), s32[]{:S(2)}) async-start(), calls=%async_computation.10 | async-start | bytes 8650752 | tf_op jit(solution)/shard_map/all_gather | solution.py:83
  55.6 35.4 %copy-start.28 = (f32[1024]{0:T(1024)}, f32[1024]{0:T(1024)S(1)}, u32[]{:S(2)}) copy-start(f32[1024]{0:T(1024)S(1)} %convert_element_type.137) | copy-start | bytes 12292
  55.6 35.4 %copy-start.25 = (f32[1024]{0:T(1024)}, f32[1024]{0:T(1024)S(1)}, u32[]{:S(2)}) copy-start(f32[1024]{0:T(1024)S(1)} %convert_element_type.136) | copy-start | bytes 12292
  57.0 12.3 %copy-start.30 = (f32[2,256]{1,0:T(2,128)}, f32[2,256]{1,0:T(2,128)S(1)}, u32[]{:S(2)}) copy-start(f32[2,256]{1,0:T(2,128)S(1)} %get-tuple-element.342) | copy-start | bytes 6148
  59.3 31.7 %copy-start.32 = (f32[1,2,2,128]{3,1,2,0:T(2,128)}, f32[1,2,2,128]{3,1,2,0:T(2,128)S(1)}, u32[]{:S(2)}) copy-start(f32[1,2,2,128]{3,1,2,0:T(2,128)S(1)} %copy.63) | copy-start | bytes 6148
  59.3 31.7 %copy-start.34 = (f32[1,2,2,128]{3,1,2,0:T(2,128)}, f32[1,2,2,128]{3,1,2,0:T(2,128)S(1)}, u32[]{:S(2)}) copy-start(f32[1,2,2,128]{3,1,2,0:T(2,128)S(1)} %copy.62) | copy-start | bytes 6148
  70.6 30.5 %copy-start.20 = (f32[2,256,8]{1,2,0:T(8,128)}, f32[2,256,8]{1,2,0:T(8,128)S(1)}, u32[]{:S(2)}) copy-start(f32[2,256,8]{1,2,0:T(8,128)S(1)} %get-tuple-element.337) | copy-start | bytes 49156
  70.6 30.5 %copy-start.22 = (f32[2,256,8]{1,2,0:T(8,128)}, f32[2,256,8]{1,2,0:T(8,128)S(1)}, u32[]{:S(2)}) copy-start(f32[2,256,8]{1,2,0:T(8,128)S(1)} %get-tuple-element.338) | copy-start | bytes 49156
  72.3 18.7 %copy-start.15 = (bf16[512,1024]{1,0:T(8,128)(2,1)}, bf16[512,1024]{1,0:T(8,128)(2,1)S(1)}, u32[]{:S(2)}) copy-start(bf16[512,1024]{1,0:T(8,128)(2,1)S(1)} %fusion.51) | copy-start | bytes 3145732
  105.9 82.2 %all-to-all-start = ((bf16[2,256,4,768]{1,0,3,2:T(2,128)(2,1)}), bf16[2,256,4,768]{1,0,3,2:T(2,128)(2,1)S(1)}, u32[]{:S(2)}, u32[]{:S(2)}) async-start(bf16[2,256,4,768]{1,0,3,2:T(2,128)(2,1)} %convert_element_type.141), calls=%async_computation | async-start | bytes 6291456 | tf_op jit(solution)/shard_map/all_to_all | solution.py:118
  109.6 493.5 %all-gather.12.cloned.1.call-start = ((), (), s32[]{:S(2)}) async-start(), calls=%async_computation.11 | async-start | bytes 8650752 | tf_op jit(solution)/shard_map/all_gather | solution.py:85
  188.1 63.3 %all-to-all-start.2 = ((bf16[2,256,4,256]{3,1,0,2:T(8,128)(2,1)}), bf16[2,256,4,256]{3,1,0,2:T(8,128)(2,1)}, u32[]{:S(2)}, u32[]{:S(2)}) async-start(bf16[2,256,4,256]{3,1,0,2:T(8,128)(2,1)} %copy.54), calls=%async_computation.2 | async-start | bytes 2097152 | tf_op jit(solution)/shard_map/all_to_all | solution.py:187
  205.5 18.8 %copy-start.18 = (bf16[2,1024,256]{1,2,0:T(8,128)(2,1)S(1)}, bf16[2,1024,256]{1,2,0:T(8,128)(2,1)}, u32[]{:S(2)}) copy-start(bf16[2,1024,256]{1,2,0:T(8,128)(2,1)} %get-tuple-element.722) | copy-start | bytes 3145732 | tf_op jit(solution)/shard_map/while
  227.8 18.8 %copy-start.18 = (bf16[2,1024,256]{1,2,0:T(8,128)(2,1)S(1)}, bf16[2,1024,256]{1,2,0:T(8,128)(2,1)}, u32[]{:S(2)}) copy-start(bf16[2,1024,256]{1,2,0:T(8,128)(2,1)} %get-tuple-element.722) | copy-start | bytes 3145732 | tf_op jit(solution)/shard_map/while
  247.6 41.8 %copy-start.8 = (bf16[2,256,1024]{2,1,0:T(8,128)(2,1)S(1)}, bf16[2,256,1024]{2,1,0:T(8,128)(2,1)}, u32[]{:S(2)}) copy-start(bf16[2,256,1024]{2,1,0:T(8,128)(2,1)} %param.23) | copy-start | bytes 3145732
  251.4 36.0 %all-to-all-start.1 = ((bf16[2,1024,1,256]{3,0,2,1:T(2,128)(2,1)}), bf16[2,1024,1,256]{3,0,2,1:T(2,128)(2,1)S(1)}, u32[]{:S(2)}, u32[]{:S(2)}) async-start(bf16[2,1024,1,256]{3,0,2,1:T(2,128)(2,1)} %bitcast.26), calls=%async_computation.1 | async-start | bytes 2097152 | tf_op jit(solution)/shard_map/all_to_all | solution.py:161
  255.9 481.2 %reduce-scatter.7.cloned.1.call-start = ((), (), s32[]{:S(2)}) async-start(), calls=%async_computation.13 | async-start | bytes 4325376 | tf_op jit(solution)/shard_map/reduce_scatter | solution.py:277
  304.7 7.8 slice-start
  305.2 7.3 slice-start.1
  333.5 7.9 slice-start
  334.0 7.4 slice-start.1
  345.9 5.0 copy-start.2
  369.8 7.9 slice-start
  370.3 7.4 slice-start.1
  382.2 4.8 copy-start.2
  398.6 7.8 slice-start
  399.1 7.3 slice-start.1
  411.0 4.8 copy-start.2
  423.1 13.6 %copy-start.23 = (f32[2,256,8]{1,2,0:T(8,128)S(1)}, f32[2,256,8]{1,2,0:T(8,128)}, u32[]{:S(2)}) copy-start(f32[2,256,8]{1,2,0:T(8,128)} %copy-done.22) | copy-start | bytes 49156
  423.1 13.6 %copy-start.4 = (bf16[2,256,1024]{2,1,0:T(8,128)(2,1)S(1)}, bf16[2,256,1024]{2,1,0:T(8,128)(2,1)}, u32[]{:S(2)}) copy-start(bf16[2,256,1024]{2,1,0:T(8,128)(2,1)} %param.21) | copy-start | bytes 3145732
  423.1 13.6 %copy-start.26 = (f32[1024]{0:T(1024)S(1)}, f32[1024]{0:T(1024)}, u32[]{:S(2)}) copy-start(f32[1024]{0:T(1024)} %copy-done.25) | copy-start | bytes 12292
  423.1 13.6 %copy-start.29 = (f32[1024]{0:T(1024)S(1)}, f32[1024]{0:T(1024)}, u32[]{:S(2)}) copy-start(f32[1024]{0:T(1024)} %copy-done.28) | copy-start | bytes 12292
  423.1 13.6 %copy-start.31 = (f32[2,256]{1,0:T(2,128)S(1)}, f32[2,256]{1,0:T(2,128)}, u32[]{:S(2)}) copy-start(f32[2,256]{1,0:T(2,128)} %copy-done.30) | copy-start | bytes 6148
  423.1 13.6 %copy-start.36 = (f32[2,256]{1,0:T(2,128)S(1)}, f32[2,256]{1,0:T(2,128)}, u32[]{:S(2)}) copy-start(f32[2,256]{1,0:T(2,128)} %get-tuple-element.339) | copy-start | bytes 6148
  432.0 80.7 %all-to-all-start.3 = ((bf16[2,1024,1,768]{3,0,2,1:T(2,128)(2,1)}), bf16[2,1024,1,768]{3,0,2,1:T(2,128)(2,1)}, u32[]{:S(2)}, u32[]{:S(2)}) async-start(bf16[2,1024,1,768]{3,0,2,1:T(2,128)(2,1)} %copy.57), calls=%async_computation.3 | async-start | bytes 6291456 | tf_op jit(solution)/shard_map/all_to_all | solution.py:246
  436.6 300.4 %reduce-scatter.5.cloned.1.call-start = ((), (), s32[]{:S(2)}) async-start(), calls=%async_computation.12 | async-start | bytes 12976128 | tf_op jit(solution)/shard_map/reduce_scatter | solution.py:275
  528.5 12.9 %copy-start.21 = (f32[2,256,8]{1,2,0:T(8,128)S(1)}, f32[2,256,8]{1,2,0:T(8,128)}, u32[]{:S(2)}) copy-start(f32[2,256,8]{1,2,0:T(8,128)} %copy-done.20) | copy-start | bytes 49156
  552.0 40.2 %copy-start.16 = (bf16[512,1024]{1,0:T(8,128)(2,1)S(1)}, bf16[512,1024]{1,0:T(8,128)(2,1)}, u32[]{:S(2)}) copy-start(bf16[512,1024]{1,0:T(8,128)(2,1)} %copy-done.15) | copy-start | bytes 3145732
  552.0 343.3 %reduce-scatter.9.cloned.1.call-start = ((), (), s32[]{:S(2)}) async-start(), calls=%async_computation.14 | async-start | bytes 17301504 | tf_op jit(solution)/shard_map/reduce_scatter | solution.py:279
  592.2 10.9 %copy-start.9 = (bf16[2,256,1024]{2,1,0:T(8,128)(2,1)S(1)}, bf16[2,256,1024]{2,1,0:T(8,128)(2,1)}, u32[]{:S(2)}) copy-start(bf16[2,256,1024]{2,1,0:T(8,128)(2,1)} %param.23) | copy-start | bytes 3145732
  640.9 442.2 %reduce-scatter.11.cloned.1.call-start = ((), (), s32[]{:S(2)}) async-start(), calls=%async_computation.15 | async-start | bytes 17301504 | tf_op jit(solution)/shard_map/reduce_scatter | solution.py:281
  660.5 8.3 copy-start.13
  668.8 8.4 copy-start.5
  668.8 8.4 copy-start.11
  668.8 8.4 copy-start.40
  732.5 351.1 %copy-start.41 = (f32[32]{0:T(128)}, f32[32]{0:T(128)S(1)}, u32[]{:S(2)}) copy-start(f32[32]{0:T(128)S(1)} %dynamic-slice.3) | copy-start | bytes 388
  (34 other events, 82.2 us)
Sparse Core Ops, SparseCore 0:
  10.9 71.9 all-gather.5
  85.8 88.0 all-gather.7
  176.7 99.3 all-gather.9
  278.8 74.7 all-gather.11
  356.2 139.9 reduce-scatter.6
  552.1 156.0 reduce-scatter.4
  711.3 184.0 reduce-scatter.8
  898.3 184.7 reduce-scatter.10
where the time goes:
time: 1100 us; the launch traced here: 1090 us
  waiting for transfers between devices  532 us (48%)
  matrix products  195 us (18%)
  blocking collectives  133 us (12%)
  local copies, waits for them, and re-layouts  127 us (12%)
  other arithmetic  56.9 us (5%)
  starting transfers between devices  17.6 us (2%)
  between operations  14.9 us (1%)
  loops' own time  14.4 us (1%)
    reduce_scatter x1, waiting for transfers between devices, local(): lax.psum_scatter(fc_out_weight_grad, ('seq', 'fsdp'), scatter_dimension=0...  188 us
    reduce_scatter x1, waiting for transfers between devices, local(): lax.psum_scatter(fc_in_weight_grad, ('seq', 'fsdp'), scatter_dimension=0,...  158 us
    unnamed x2, blocking collectives  83.5 us
    all_to_all x1, waiting for transfers between devices, local(): lax.all_to_all(stacked.reshape(local_seqs, length, 1, per_group * 3 * HD)...  75.5 us
    all_gather x1, waiting for transfers between devices, local(): lax.all_gather(out_weight, ('seq', 'fsdp'), axis=0, tiled=True)  63.6 us
    dot_general x4, matrix products, times_transposed(): lax.dot_general(left, right, (((1,), (1,)), ((), ())), preferred_element_...  49.8 us
    all_gather x1, blocking collectives, local(): lax.all_gather(fc_in_bias, ('seq', 'fsdp'), axis=0, tiled=True)  39.5 us
    dot_general x4, matrix products, backward_step(): jnp.einsum('qhd,khd->hqk', query_rows, key_everywhere, preferred_element_...  29.2 us
  transfers between devices with their start and end apart: 12, of which 7 were waited for; matrix products, arithmetic and copies ran while one was open for 32% of the time, Pallas kernels for 0%

commit v1 on v0

v1 whole, which is shorter than its diff:
```python
from functools import partial
import math

import jax
import jax.numpy as jnp
import numpy as np
from jax import lax
from jax.experimental import pallas as pl
from jax.experimental.pallas import tpu as pltpu
from jax.sharding import PartitionSpec as P

D = 1024
H = 16
HD = 64
ROT = 16
GROUPS = 4
BF = jnp.bfloat16
F32 = jnp.float32


def dot(left, right):
    return jnp.dot(left, right, preferred_element_type=F32)


def outer_product(left, right):
    return lax.dot_general(left, right, (((0,), (0,)), ((), ())), preferred_element_type=F32)


def times_transposed(left, right):
    return lax.dot_general(left, right, (((1,), (1,)), ((), ())), preferred_element_type=F32)


def swap(value, axis, bit):
    return lax.ppermute(value, axis, [(i, i ^ bit) for i in range(lax.axis_size(axis))])


def shift(value, by):
    count = lax.axis_size("seq")
    return lax.ppermute(
        value, "seq", [(i, i + by) for i in range(count) if 0 <= i + by < count]
    )


def far_bits(count):
    bits = []
    while count > 1:
        count //= 2
        bits.append(count)
    return bits


class Clock:
    def __init__(self, token):
        self.token = token

    def gate(self, *values):
        return lax.optimization_barrier((values, self.token))[0]

    def tick(self, *values):
        self.token = lax.optimization_barrier((self.token, values))[0]


class Chips:
    def __init__(self):
        self.nz, self.nf = lax.axis_size("seq"), lax.axis_size("fsdp")
        self.per = self.nf // 2
        self.count = self.nz * self.per
        self.core = lax.axis_index("fsdp") % 2
        self.me = lax.axis_index("seq") * self.per + lax.axis_index("fsdp") // 2
        self.line = [bit * self.per for bit in far_bits(self.nz)]
        self.plane = list(reversed(far_bits(self.per)))
        self.cube = len(self.plane) == 2 and self.nz == 4
        far, near = self.line[0], self.line[-1]
        if self.cube:
            bx, by = self.plane
            a, b = [0, far], [near, near ^ far]

            def over(chips, to):
                return [chip ^ to for chip in chips]

            ax, yb = a + over(a, bx), b + over(b, by)
            self.pieces = [ax, yb, over(ax, by), over(yb, bx)]
        else:
            order = [0]
            for bit in self.line + self.plane:
                order = order + [chip ^ bit for chip in order]
            self.pieces = [order]
        self.order = sum(self.pieces, [])

    def places(self):
        return jnp.asarray(np.array(self.order, np.int32)) ^ self.me

    def spots(self):
        place = np.zeros(self.count, np.int32)
        place[self.order] = np.arange(self.count)
        return jnp.asarray(place)[jnp.arange(self.count, dtype=jnp.int32) ^ self.me]

    def cross(self, value, bit):
        if bit >= self.per:
            return swap(value, "seq", bit // self.per)
        return swap(value, "fsdp", bit * 2)

    def other_core(self, value):
        return swap(value, "fsdp", 1)

    def both(self, mine, other):
        first = self.core == 0
        return jnp.where(first, mine, other), jnp.where(first, other, mine)

    def pick(self, halves):
        first = self.core == 0
        return jnp.where(first, halves[0], halves[1]), jnp.where(first, halves[1], halves[0])


class Gather:
    def __init__(self, chips, shard):
        self.chips = chips
        self.parts = {"s": shard}

    def jobs(self, stage):
        chips, parts = self.chips, self.parts
        if not chips.cube:
            return []
        far, near = chips.line
        bx, by = chips.plane
        if stage == "near":
            parts["a"] = jnp.concatenate([parts["s"], parts["f"]], axis=0)
        if stage == "second":
            parts["ax"] = jnp.concatenate([parts["a"], parts["xa"]], axis=0)
            parts["by"] = jnp.concatenate([parts["b"], parts["yb"]], axis=0)
        return {
            "far": [("f", "s", far)],
            "near": [("b", "a", near)],
            "first": [("xa", "a", bx), ("yb", "b", by)],
            "second": [("yax", "ax", by), ("xby", "by", bx)],
        }[stage]

    def pieces(self):
        if not self.chips.cube:
            value = self.parts["s"]
            for bit in self.chips.line + self.chips.plane:
                value = jnp.concatenate([value, self.chips.cross(value, bit)], axis=0)
            return [value]
        return [self.parts[name] for name in ("ax", "by", "yax", "xby")]


class Scatter:
    def __init__(self, chips, pieces):
        self.chips = chips
        self.parts = dict(zip(("ax", "by", "yax", "xby"), pieces))

    def jobs(self, stage):
        chips, parts = self.chips, self.parts
        if not chips.cube:
            return []
        far, near = chips.line
        bx, by = chips.plane

        def total(name, *more):
            value = parts[name].astype(F32)
            for other in more:
                value = value + parts[other].astype(F32)
            return value

        half = parts["ax"].shape[0] // 2
        if stage == "second":
            value = total("ax", "r_yax")
            parts["a"], parts["xa"] = value[:half].astype(BF), value[half:].astype(BF)
            value = total("by", "r_xby")
            parts["b"], parts["yb"] = value[:half].astype(BF), value[half:].astype(BF)
        if stage == "near":
            parts["b"] = total("b", "r_yb").astype(BF)
        if stage == "far":
            value = total("a", "r_xa", "r_b")
            parts["keep"] = value[: half // 2]
            parts["send"] = value[half // 2 :].astype(BF)
        return {
            "first": [("r_yax", "yax", by), ("r_xby", "xby", bx)],
            "second": [("r_xa", "xa", bx), ("r_yb", "yb", by)],
            "near": [("r_b", "b", near)],
            "far": [("r_far", "send", far)],
        }[stage]

    def result(self):
        if not self.chips.cube:
            total = self.parts["ax"].astype(F32)
            for bit in reversed(self.chips.line + self.chips.plane):
                half = total.shape[0] // 2
                total = total[:half] + self.chips.cross(total[half:].astype(BF), bit).astype(F32)
            return total
        return self.parts["keep"] + self.parts["r_far"].astype(F32)


def cost(flops, bytes_accessed, transcendentals=0):
    return pl.CostEstimate(
        flops=flops, bytes_accessed=bytes_accessed, transcendentals=transcendentals
    )


def turn(value, cosine, forth, back):
    return (
        value * cosine
        + pltpu.roll(value, 128 - ROT // 2, 1) * forth
        + pltpu.roll(value, ROT // 2, 1) * back
    )


def tables_kernel(place_ref, speed_ref, forth_ref, back_ref, cos_ref, to_ref, from_ref):
    angle = place_ref[...].astype(F32) * speed_ref[...]
    cos_ref[...] = jnp.cos(angle)
    sine = jnp.sin(angle)
    to_ref[...] = sine * forth_ref[...]
    from_ref[...] = sine * back_ref[...]


def rope_tables(positions):
    half = ROT // 2
    inverse = 1.0 / 10000.0 ** (jnp.arange(0, ROT, 2, dtype=F32) / ROT)
    speed = jnp.concatenate([inverse, inverse, jnp.zeros((HD - ROT,), F32)])
    speed = jnp.concatenate([speed, speed]).reshape(1, 128)
    lanes = np.arange(128) % HD
    forth = -(lanes < half).astype(np.float32)[None, :]
    back = ((lanes >= half) & (lanes < ROT)).astype(np.float32)[None, :]
    rows = positions.shape[0]
    return pl.pallas_call(
        tables_kernel,
        out_shape=(jax.ShapeDtypeStruct((rows, 128), F32),) * 3,
        cost_estimate=cost(rows * 128 * 100, rows * 128 * 16),
        name="tables",
    )(positions.reshape(rows, 1), speed, jnp.asarray(forth), jnp.asarray(back))


def stack(refs):
    return jnp.concatenate([ref[...] for ref in refs], axis=0) if len(refs) > 1 else refs[0][...]


def project_kernel(count, normed_ref, bias_ref, cos_ref, forth_ref, back_ref, *refs):
    q_ref, kv_ref = refs[count:]
    value = dot(normed_ref[...], stack(refs[:count])) + bias_ref[...]
    tables = cos_ref[...], forth_ref[...], back_ref[...]
    q_ref[...] = turn(value[:, :128], *tables).astype(BF)
    kv_ref[:, :128] = turn(value[:, 128:256], *tables).astype(BF)
    kv_ref[:, 128:] = value[:, 256:].astype(BF)


def project(normed, pieces, bias, tables, group):
    rows = normed.shape[0]
    step = 512
    table = pl.BlockSpec((step, 128), lambda i: (i, 0))
    return pl.pallas_call(
        partial(project_kernel, len(pieces)),
        grid=(rows // step,),
        out_shape=(
            jax.ShapeDtypeStruct((rows, 128), BF),
            jax.ShapeDtypeStruct((rows, 256), BF),
        ),
        in_specs=[
            pl.BlockSpec((step, D), lambda i: (i, 0)),
            pl.BlockSpec((1, 384), lambda i: (0, group)),
            table,
            table,
            table,
        ]
        + [pl.BlockSpec((piece.shape[0], 384), lambda i: (0, group)) for piece in pieces],
        out_specs=(
            pl.BlockSpec((step, 128), lambda i: (i, 0)),
            pl.BlockSpec((step, 256), lambda i: (i, 0)),
        ),
        cost_estimate=cost(2 * rows * D * 384, 2 * (rows * D + D * 384 + rows * 384)),
        name="project",
    )(normed, bias, *tables, *pieces)


def attend_kernel(chunks, q_ref, do_ref, ql_ref, kl_ref, *refs):
    kv_refs = refs[:chunks]
    o_ref, dq_ref = refs[chunks : chunks + 2]
    dkv_refs = refs[chunks + 2 : 2 * chunks + 2]
    bias_ref = refs[-1]
    rows = q_ref.shape[0]
    for chunk in range(chunks):
        old = (chunks - 1 - chunk) * rows
        same = kl_ref[0, old : old + rows, :] == ql_ref[0]
        if chunk == 0:
            key = lax.broadcasted_iota(jnp.int32, (rows, rows), 0)
            query = lax.broadcasted_iota(jnp.int32, (rows, rows), 1)
            same = same & (key <= query)
        bias_ref[chunk * rows : (chunk + 1) * rows, :] = jnp.where(same, 0.0, -1e30)

    keys = jnp.concatenate([ref[:, :128] for ref in kv_refs], axis=0)
    values = jnp.concatenate([ref[:, 128:] for ref in kv_refs], axis=0)
    keys_t = keys.T
    values_t = values.T
    scaled = q_ref[...] * 0.125
    given = do_ref[...]
    lane = lax.broadcasted_iota(jnp.int32, (rows, 128), 1)
    out_t, dq_t, probs_all, ds_all, q_all, g_all = [], [], [], [], [], []
    for head in range(2):
        mine = (lane < HD) if head == 0 else (lane >= HD)
        query = jnp.where(mine, scaled, jnp.zeros_like(scaled))
        grad = jnp.where(mine, given, jnp.zeros_like(given))
        part = slice(head * HD, (head + 1) * HD)
        scores = times_transposed(keys, query) + bias_ref[...]
        top = jnp.max(scores, axis=0, keepdims=True)
        unscaled = jnp.exp(scores - top)
        total = jnp.sum(unscaled, axis=0, keepdims=True)
        probs = unscaled * (1.0 / total)
        rounded = probs.astype(BF)
        out_t.append(dot(values_t[part], rounded))
        prob_grad = times_transposed(values, grad)
        inner = jnp.sum(probs * prob_grad, axis=0, keepdims=True)
        score_grad = (probs * (prob_grad - inner)).astype(BF)
        dq_t.append(dot(keys_t[part], score_grad))
        probs_all.append(rounded)
        ds_all.append(score_grad)
        q_all.append(query)
        g_all.append(grad)
    o_ref[...] = jnp.concatenate(out_t, axis=0).T.astype(BF)
    dq_ref[...] = (jnp.concatenate(dq_t, axis=0).T * 0.125).astype(BF)
    dk = dot(jnp.concatenate(ds_all, axis=1), jnp.concatenate(q_all, axis=0))
    dv = dot(jnp.concatenate(probs_all, axis=1), jnp.concatenate(g_all, axis=0))
    for chunk, ref in enumerate(dkv_refs):
        ref[:, :128] = dk[chunk * rows : (chunk + 1) * rows].astype(ref.dtype)
        ref[:, 128:] = dv[chunk * rows : (chunk + 1) * rows].astype(ref.dtype)


def attend(group, seqs, query, grad, query_labels, key_labels, kvs):
    chunks = len(kvs)
    total, width = query.shape
    rows = total // seqs
    keys = rows * chunks
    narrow = pl.BlockSpec((rows, 128), lambda b: (b, 0))
    wide = pl.BlockSpec((rows, 256), lambda b: (b, 0))
    return pl.pallas_call(
        partial(attend_kernel, chunks),
        grid=(seqs,),
        out_shape=(
            jax.ShapeDtypeStruct((total, 128), BF),
            jax.ShapeDtypeStruct((total, 128), BF),
            jax.ShapeDtypeStruct((total, 256), F32),
        )
        + (jax.ShapeDtypeStruct((total, 256), BF),) * (chunks - 1),
        in_specs=[
            narrow,
            pl.BlockSpec((rows, 128), lambda b: (b, group)),
            pl.BlockSpec((1, 1, rows), lambda b: (b, 0, 0)),
            pl.BlockSpec((1, keys, 1), lambda b: (b, 0, 0)),
        ]
        + [
            pl.BlockSpec((rows, 256), lambda b, place=place: (b + place * seqs, 0))
            for _, place in kvs
        ],
        out_specs=(narrow, narrow) + (wide,) * chunks,
        scratch_shapes=[pltpu.VMEM((keys, rows), F32)],
        cost_estimate=cost(
            24 * seqs * rows * keys * 128, total * 256 * (3 + 5 * chunks), seqs * 2 * rows * keys
        ),
        name="attend",
    )(query, grad, query_labels, key_labels, *[array for array, _ in kvs])


def unturn_kernel(dq_ref, own_ref, more_ref, cos_ref, forth_ref, back_ref, out_ref):
    cosine, forth, back = cos_ref[...], -forth_ref[...], -back_ref[...]
    kv = (own_ref[...] + more_ref[...].astype(F32)).astype(BF)
    out_ref[:, :128] = turn(dq_ref[...].astype(F32), cosine, forth, back).astype(BF)
    out_ref[:, 128:256] = turn(kv[:, :128].astype(F32), cosine, forth, back).astype(BF)
    out_ref[:, 256:] = kv[:, 128:]


def unturn(dq, own, more, place, tables):
    rows = dq.shape[0]
    step = rows // 2

    def spec(columns, first=0):
        return pl.BlockSpec((step, columns), lambda i: (i + first, 0))

    return pl.pallas_call(
        unturn_kernel,
        grid=(rows // step,),
        out_shape=jax.ShapeDtypeStruct((rows, 384), BF),
        in_specs=[spec(128), spec(256), spec(256, place * 2)] + [spec(128)] * 3,
        out_specs=spec(384),
        cost_estimate=cost(rows * 128 * 20, rows * 128 * 26),
        name="unturn",
    )(dq, own, more, *tables)


ROOT_HALF = math.sqrt(0.5)
DENSITY = 1.0 / math.sqrt(2.0 * math.pi)


def gelu_and_slope(value):
    share = 0.5 + 0.5 * lax.erf(value * ROOT_HALF)
    return value * share, share + value * (DENSITY * jnp.exp(-0.5 * value * value))


def hidden_kernel(count, normed_ref, bias_ref, *refs):
    act_ref, act_t_ref, slope_ref = refs[count:]
    rows = 256
    weight = stack(refs[:count])

    def some(i, carry):
        here = pl.ds(pl.multiple_of(i * rows, rows), rows)
        value = dot(normed_ref[here, :], weight) + bias_ref[...]
        act, slope = gelu_and_slope(value)
        act = act.astype(BF)
        act_ref[here, :] = act
        act_t_ref[:, here] = act.T
        slope_ref[here, :] = slope
        return carry

    lax.fori_loop(0, normed_ref.shape[0] // rows, some, 0)


def hidden(normed, pieces, bias):
    rows, width = normed.shape[0], bias.shape[1]
    return pl.pallas_call(
        partial(hidden_kernel, len(pieces)),
        grid=(width // 256,),
        out_shape=(
            jax.ShapeDtypeStruct((rows, width), BF),
            jax.ShapeDtypeStruct((width, rows), BF),
            jax.ShapeDtypeStruct((rows, width), F32),
        ),
        in_specs=[
            pl.BlockSpec((rows, D), lambda j: (0, 0)),
            pl.BlockSpec((1, 256), lambda j: (0, j)),
        ]
        + [pl.BlockSpec((piece.shape[0], 256), lambda j: (0, j)) for piece in pieces],
        out_specs=(
            pl.BlockSpec((rows, 256), lambda j: (0, j)),
            pl.BlockSpec((256, rows), lambda j: (j, 0)),
            pl.BlockSpec((rows, 256), lambda j: (0, j)),
        ),
        cost_estimate=cost(2 * rows * D * width + 50 * rows * width, 9 * rows * width),
        name="hidden",
    )(normed, bias, *pieces)


def mlp_kernel(rels, me_ref, g_ref, act_ref, slope_ref, *refs):
    count = len(rels)
    hg_ref, sum_ref, out_ref, w_ref, sem = refs[count:]
    j = pl.program_id(0)
    rows = 256

    @pl.when(j == 0)
    def _():
        copies = []
        for piece, chips in zip(refs[:count], rels):
            for place, rel in enumerate(chips):
                first = pl.multiple_of((me_ref[0] ^ rel) * 128, 128)
                copies.append(
                    pltpu.make_async_copy(
                        piece.at[pl.ds(place * 128, 128), :], w_ref.at[pl.ds(first, 128), :], sem
                    )
                )
        for copy in copies:
            copy.start()
        out_ref[...] = jnp.zeros_like(out_ref)
        for copy in copies:
            copy.wait()

    w = w_ref[pl.ds(pl.multiple_of(j * 256, 256), 256), :]

    def some(i, total):
        here = pl.ds(pl.multiple_of(i * rows, rows), rows)
        grad = (times_transposed(g_ref[here, :], w) * slope_ref[here, :]).astype(BF)
        hg_ref[here, :] = grad
        out_ref[here, :] += dot(act_ref[here, :], w)
        return total + jnp.sum(grad.astype(F32), axis=0, keepdims=True)

    sum_ref[...] = lax.fori_loop(0, g_ref.shape[0] // rows, some, jnp.zeros((1, 256), F32))


def mlp(chips, grad, act, slope, pieces):
    rows, width = act.shape
    return pl.pallas_call(
        partial(mlp_kernel, chips.pieces),
        grid=(width // 256,),
        out_shape=(
            jax.ShapeDtypeStruct((rows, width), BF),
            jax.ShapeDtypeStruct((1, width), F32),
            jax.ShapeDtypeStruct((rows, D), F32),
        ),
        in_specs=[
            pl.BlockSpec(memory_space=pltpu.SMEM),
            pl.BlockSpec((rows, D), lambda j: (0, 0)),
            pl.BlockSpec((rows, 256), lambda j: (0, j)),
            pl.BlockSpec((rows, 256), lambda j: (0, j)),
        ]
        + [pl.BlockSpec(memory_space=pl.ANY)] * len(pieces),
        out_specs=(
            pl.BlockSpec((rows, 256), lambda j: (0, j)),
            pl.BlockSpec((1, 256), lambda j: (0, j)),
            pl.BlockSpec((rows, D), lambda j: (0, 0)),
        ),
        scratch_shapes=[pltpu.VMEM((width, D), BF), pltpu.SemaphoreType.DMA],
        cost_estimate=cost(4 * rows * D * width, 10 * rows * width),
        name="mlp",
    )(chips.me.reshape(1), grad, act, slope, *pieces)


def row_grads_kernel(heights, steps, left_ref, right_ref, *refs):
    out_refs = refs[-len(heights) :]
    more_refs = refs[: -len(heights)]

    @pl.when(pl.program_id(0) < steps)
    def _():
        value = dot(left_ref[...], right_ref[...])
        first = 0
        for height, ref in zip(heights, out_refs):
            ref[...] = value[first : first + height].astype(BF)
            first += height

    if more_refs:

        @pl.when(pl.program_id(0) >= steps)
        def _():
            first = 0
            for height, ref in zip(heights, out_refs):
                ref[...] = more_refs[0][first : first + height, :]
                first += height


def row_grads(chips, left, right, more=None):
    rows, tokens = left.shape
    heights = [rows // len(chips.pieces)] * len(chips.pieces)
    step = 256
    steps = right.shape[1] // step
    columns = right.shape[1] + (0 if more is None else more.shape[1])
    last = steps - 1
    return pl.pallas_call(
        partial(row_grads_kernel, heights, steps),
        grid=(columns // step,),
        out_shape=tuple(jax.ShapeDtypeStruct((height, columns), BF) for height in heights),
        in_specs=[
            pl.BlockSpec((rows, tokens), lambda j: (0, 0)),
            pl.BlockSpec((tokens, step), lambda j: (0, jnp.minimum(j, last))),
        ]
        + (
            []
            if more is None
            else [pl.BlockSpec((rows, step), lambda j: (0, jnp.maximum(j - steps, 0)))]
        ),
        out_specs=tuple(pl.BlockSpec((height, step), lambda j: (0, j)) for height in heights),
        cost_estimate=cost(2 * rows * tokens * columns, 2 * (rows * tokens + rows * columns)),
        name="row_grads",
    )(left, right, *([] if more is None else [more]))


def unit_grads_kernel(pieces, order_ref, *refs):
    lefts, right_ref, out_refs = refs[:4], refs[4], refs[5:]
    value = dot(stack(lefts), right_ref[...]).astype(BF)
    for piece in range(pieces):

        @pl.when(pl.program_id(0) == piece)
        def _(piece=piece):
            out_refs[piece][...] = value


def unit_grads(chips, left, right):
    tokens = left.shape[1]
    columns = right.shape[1]
    pieces = len(chips.pieces)

    def block(place):
        return pl.BlockSpec((128, tokens), lambda k, order: (order[4 * k + place], 0))

    return pl.pallas_call(
        partial(unit_grads_kernel, pieces),
        out_shape=tuple(jax.ShapeDtypeStruct((512, columns), BF) for _ in range(pieces)),
        grid_spec=pltpu.PrefetchScalarGridSpec(
            num_scalar_prefetch=1,
            grid=(pieces,),
            in_specs=[block(place) for place in range(4)]
            + [pl.BlockSpec((tokens, columns), lambda k, order: (0, 0))],
            out_specs=tuple(
                pl.BlockSpec((512, columns), lambda k, order: (0, 0)) for _ in range(pieces)
            ),
        ),
        cost_estimate=cost(2 * tokens * columns * 512 * pieces, 4 * 512 * pieces * columns),
        name="unit_grads",
    )(chips.places(), left, left, left, left, right)


def norm_grad_kernel(count, qkv_ref, hidden_ref, *refs):
    out_ref = refs[-1]
    first = 0
    wide, tall = qkv_ref.shape[1], hidden_ref.shape[1]
    for one, two in zip(refs[:count], refs[count : 2 * count]):
        rows = one.shape[0]
        out_ref[:, first : first + rows] = times_transposed(
            qkv_ref[...], one[:, :wide]
        ) + times_transposed(hidden_ref[...], two[:, :tall])
        first += rows


def norm_grad(projected_grad, hidden_grad, qkv_pieces, in_pieces):
    rows = projected_grad.shape[0]
    step = 256

    def whole(piece):
        return pl.BlockSpec(piece.shape, lambda i: (0, 0))

    return pl.pallas_call(
        partial(norm_grad_kernel, len(qkv_pieces)),
        grid=(rows // step,),
        out_shape=jax.ShapeDtypeStruct((rows, D), F32),
        in_specs=[
            pl.BlockSpec((step, projected_grad.shape[1]), lambda i: (i, 0)),
            pl.BlockSpec((step, hidden_grad.shape[1]), lambda i: (i, 0)),
        ]
        + [whole(piece) for piece in qkv_pieces + in_pieces],
        out_specs=pl.BlockSpec((step, D), lambda i: (i, 0)),
        cost_estimate=cost(7 * rows * D * D, 12 * rows * D),
        name="norm_grad",
    )(projected_grad, hidden_grad, *qkv_pieces, *in_pieces)


def local(
    hidden_in,
    document_labels,
    cotangent,
    ln_gain,
    ln_bias,
    qkv_weight,
    qkv_bias,
    out_weight,
    out_bias,
    fc_in_weight,
    fc_in_bias,
    fc_out_weight,
    fc_out_bias,
):
    chips = Chips()
    count, core, nz = chips.count, chips.core, chips.nz
    both, pick = chips.both, chips.pick
    local_seqs, tok_count = hidden_in.shape[:2]
    length = tok_count * nz
    row_count = local_seqs * tok_count
    seqs = 2 * local_seqs
    d_rows = qkv_weight.shape[0]
    f_rows = fc_out_weight.shape[0]
    units = fc_in_weight.shape[1] // 2
    pair = H // 2 // GROUPS
    reach = -(-(length // 2 - 1) // tok_count)
    smooth = chips.cube and f_rows == 128 and reach == 2

    x_own = hidden_in.reshape(row_count, D)
    g_own = cotangent.reshape(row_count, D)
    vectors = (ln_gain, ln_bias, qkv_bias, out_bias, fc_in_bias, fc_out_bias)
    marks = (document_labels + 1).astype(BF).reshape(-1)
    sides = [vector.reshape(-1, d_rows).T for vector in vectors + (marks,)]
    widths = [side.shape[1] for side in sides]
    side_width = 128 * (-(-sum(widths) // 128))
    side = jnp.pad(jnp.concatenate(sides, axis=1), ((0, 0), (0, side_width - sum(widths))))
    qkv_keep, qkv_give = pick(
        qkv_weight.reshape(d_rows, 2, GROUPS, pair, 3, HD)
        .transpose(1, 0, 2, 4, 3, 5)
        .reshape(2, d_rows, 3 * D // 2)
    )
    in_keep, in_give = pick(
        fc_in_weight.reshape(d_rows, count, 2, f_rows)
        .transpose(2, 0, 1, 3)
        .reshape(2, d_rows, units)
    )
    qkv_wide = 3 * D // 2
    clock = Clock(side[:1])
    box = {}

    def slot(jobs, work=None, *inputs):
        gated, given = clock.gate(tuple(job[2] for job in jobs), inputs)
        results = [job[3](value) for job, value in zip(jobs, gated)]
        made = work(*given) if work is not None else ()
        clock.tick(results, made)
        for job, value in zip(jobs, results):
            job[0][job[1]] = value
        return made

    def moves(line, stage):
        return [
            (line.parts, name, line.parts[source], partial(chips.cross, bit=bit))
            for name, source, bit in line.jobs(stage)
        ]

    def core_move(name, value):
        return (box, name, value, chips.other_core)

    block = 2 * d_rows
    wanted = jnp.repeat(chips.places(), block, total_repeat_length=D) * block + jnp.asarray(
        np.arange(D, dtype=np.int32) % block
    )

    def choice(wanted):
        return (jnp.arange(D, dtype=jnp.int32)[:, None] == wanted[None, :]).astype(BF)

    chosen = slot(
        [
            core_move("give", jnp.concatenate([qkv_give, side, in_give], axis=1)),
            core_move("x", x_own),
        ],
        choice,
        wanted,
    )
    keep = jnp.concatenate([qkv_keep, side, in_keep], axis=1)
    full = jnp.concatenate(both(keep, box["give"]), axis=0)
    folded = jnp.concatenate([out_weight[:, : D // 2], out_weight[:, D // 2 :]], axis=0)
    line_a = Gather(chips, full[:, : qkv_wide + side_width])
    line_b = Gather(chips, jnp.concatenate([full[:, qkv_wide + side_width :], folded], axis=1))
    line_c = Gather(chips, fc_out_weight)
    x_both = jnp.concatenate([x_own, box["x"]], axis=0)

    def prepare(x, chosen):
        x = dot(x, chosen)
        average = jnp.mean(x, axis=-1, keepdims=True)
        centered = x - average
        spread = jnp.mean(centered * centered, axis=-1, keepdims=True)
        inv_std = lax.rsqrt(spread + 1e-05)
        return centered * inv_std, inv_std

    xhat, inv_std = slot(
        moves(line_a, "far") + [core_move("g", g_own)], prepare, x_both, chosen
    )
    g_both = jnp.concatenate([g_own, box["g"]], axis=0)
    grad_sum = slot(
        moves(line_a, "near") + moves(line_b, "far"),
        lambda g: jnp.sum(g.astype(F32), axis=0),
        g_own,
    )

    def split_side(rows):
        values = rows[:, qkv_wide : qkv_wide + side_width]
        parts = []
        first = 0
        for width in widths:
            parts.append(values[:, first : first + width])
            first += width
        return parts

    def line_marks(*rows):
        if chips.cube:
            rows = jnp.concatenate(rows, axis=0)
            order = chips.pieces[0][:2] + chips.pieces[1][:2]
            spot = np.zeros(nz, np.int32)
            spot[[chip // chips.per for chip in order]] = np.arange(nz)
            place = lax.axis_index("seq")
            values = split_side(rows)[-1].reshape(nz, 2, d_rows, -1)
            values = values[jnp.asarray(spot)[jnp.arange(nz, dtype=jnp.int32) ^ place]]
            values = values.transpose(0, 1, 3, 2).reshape(nz, 2, local_seqs, tok_count)
        else:
            own = document_labels + 1
            values = jnp.stack(
                [
                    lax.all_gather(labels, "seq", axis=0)
                    for labels in both(own, chips.other_core(own))
                ],
                axis=1,
            )
        values = jnp.stack(pick(values.transpose(1, 0, 2, 3)), axis=0)
        values = values.transpose(0, 2, 1, 3).reshape(seqs, length).astype(jnp.int32)
        values = jnp.pad(values, ((0, 0), (reach * tok_count, 0)))
        seen = lax.dynamic_slice_in_dim(
            values, lax.axis_index("seq") * tok_count, (reach + 1) * tok_count, 1
        )
        mine = seen[:, reach * tok_count :]
        order_of = jnp.arange((reach + 1) * tok_count, dtype=jnp.int32) - reach * tok_count
        places = jnp.arange(tok_count, dtype=jnp.int32)
        earlier = (seen[:, None, :] == mine[:, :, None]) & (
            order_of[None, None, :] < places[None, :, None]
        )
        positions = jnp.sum(earlier.astype(jnp.int32), axis=-1).reshape(seqs * tok_count)
        return rope_tables(positions), seen[:, :, None], mine[:, None, :]

    tables, key_labels, query_labels = slot(
        moves(line_a, "first") + moves(line_b, "near") + moves(line_c, "far"),
        line_marks,
        *([line_a.parts["a"], line_a.parts["b"]] if chips.cube else []),
    )
    slot(moves(line_a, "second") + moves(line_c, "near"))
    qkv_pieces = line_a.pieces()

    def parameters(*pieces):
        rows = jnp.concatenate(
            [piece[:, qkv_wide : qkv_wide + side_width] for piece in pieces], axis=0
        ).T.astype(F32)
        spots = chips.spots()
        ours = rows[: sum(widths[:-1])].reshape(-1, count, 2, d_rows)[:, spots]
        values = []
        first = 0
        for width in widths[:-1]:
            value = ours[first : first + width]
            values.append(value.transpose(1, 2, 0, 3).reshape(count * block * width))
            first += width
        b_qkv, b_out, b_in, b_fc = values[2:]
        b_qkv = pick(
            b_qkv.reshape(2, GROUPS, pair, 3, HD).transpose(0, 1, 3, 2, 4).reshape(2, 1, qkv_wide)
        )[0]
        b_in = pick(b_in.reshape(count, 2, f_rows).transpose(1, 0, 2).reshape(2, 1, units))[0]
        return rows[0:1], rows[1:2], b_qkv, b_out + b_fc, b_in

    def start_work(xhat, pieces, tables):
        gain, norm_shift, b_qkv, b_rows, b_in = parameters(*pieces)
        normed = (xhat * gain + norm_shift).astype(BF)
        return gain, b_rows, b_in, b_qkv, normed, project(normed, pieces, b_qkv, tables, 0)

    gain, b_rows, b_in, b_qkv, normed, first_pair = slot(
        moves(line_b, "first"), start_work, xhat, qkv_pieces, tables
    )
    queries, own_kvs = {0: first_pair[0]}, {0: first_pair[1]}
    hops, backs, sent = {}, {}, {}
    total_rows = seqs * tok_count

    def hop(step):
        parts = []
        if step > 0:
            last = hops[step - 1]
            parts.append(last[-total_rows:])
        if step < GROUPS:
            parts.append(own_kvs[step])
        value = parts[0] if len(parts) == 1 else jnp.concatenate(parts, axis=0)
        return (hops, step, value, partial(shift, by=1))

    def seen_kvs(group):
        if not smooth:
            found = [(own_kvs[group], 0)]
            for _ in range(reach):
                found.append((shift(found[-1][0], 1), 0))
            return found
        return [
            (own_kvs[group], 0),
            (hops[group], 0 if group == 0 else 1),
            (hops[group + 1], 0),
        ]

    def hop_jobs(step):
        return [hop(step)] if smooth else []

    results = {}

    def back(step):
        parts = []
        if step > 0:
            last = backs[step - 1][-total_rows:]
            value = results[step - 1][3].astype(F32) + last.astype(F32)
            parts.append(value.astype(BF))
        if step < GROUPS:
            parts.append(results[step][4])
        value = parts[0] if len(parts) == 1 else jnp.concatenate(parts, axis=0)
        return (backs, step, value, partial(shift, by=-1))

    def back_jobs(step):
        return [back(step)] if smooth else []

    def returned(group):
        if smooth:
            return backs[group + 1], 0
        value = shift(results[group][-1], -1)
        for step in range(reach - 1, 0, -1):
            value = (results[group][2 + step].astype(F32) + value.astype(F32)).astype(BF)
            value = shift(value, -1)
        return value, 0

    def projections(groups):
        def work(normed, pieces, b_qkv, tables):
            return [project(normed, pieces, b_qkv, tables, group) for group in groups], normed.T

        return work

    made, normed_t = slot(
        moves(line_b, "second") + hop_jobs(0),
        projections((1, 2, 3)),
        normed,
        qkv_pieces,
        b_qkv,
        tables,
    )
    for group in (1, 2, 3):
        queries[group], own_kvs[group] = made[group - 1]
    in_pieces = line_b.pieces()

    def my_rows(*pieces):
        rows = jnp.concatenate([piece[:, units:] for piece in pieces], axis=0)
        rows = rows.reshape(count, 2, d_rows, D // 2).transpose(0, 2, 1, 3)
        return rows.reshape(count, d_rows, D)[chips.spots()]

    def units_of(normed, b_in, *pieces):
        if smooth:
            return hidden(normed, pieces, b_in)
        act, slope = gelu_and_slope(dot(normed, stack_arrays(pieces)[:, :units]) + b_in)
        act = act.astype(BF)
        return act, act.T, slope

    def stack_arrays(pieces):
        return jnp.concatenate(pieces, axis=0)

    out_mine = slot(moves(line_c, "first") + hop_jobs(1), my_rows, *in_pieces)
    act, act_t, slope = slot(
        [core_move("out", out_mine)] + hop_jobs(2), units_of, normed, b_in, *in_pieces
    )
    out_heads = pick(jnp.stack(both(out_mine, box["out"]), axis=1).reshape(2, D // 2, D))[0]

    def attention(group):
        def work(query, context_grad, query_labels, key_labels, *arrays):
            kvs = [(array, place) for array, (_, place) in zip(arrays, found)]
            return attend(group, seqs, query, context_grad, query_labels, key_labels, kvs)

        found = seen_kvs(group)
        return (work, queries[group], context_grad, query_labels, key_labels) + tuple(
            array for array, _ in found
        )

    def grad_of_context(g_both, out_heads):
        return times_transposed(g_both, out_heads).astype(BF)

    context_grad = grad_of_context(g_both, out_heads)
    results[0] = slot(moves(line_c, "second") + hop_jobs(3), *attention(0))
    fc_pieces = line_c.pieces()

    def fc_out_grad(act_t, g_both):
        if smooth:
            return unit_grads(chips, act_t, g_both)
        rows = act_t.reshape(count, f_rows, act_t.shape[1])[chips.places()]
        return [dot(rows.reshape(units, -1), g_both).astype(BF)]

    sum_fc = Scatter(
        chips, slot(hop_jobs(4) + back_jobs(0), fc_out_grad, act_t, g_both)
    )
    results[1] = slot(moves(sum_fc, "first"), *attention(1))

    def mlp_work(g_both, act, slope, *pieces):
        if smooth:
            return mlp(chips, g_both, act, slope, pieces)
        weight = stack_arrays(pieces).reshape(count, f_rows, D)[chips.spots()].reshape(units, D)
        grad = (times_transposed(g_both, weight) * slope).astype(BF)
        total = jnp.sum(grad.astype(F32), axis=0, keepdims=True)
        return grad, total, dot(act, weight)

    hidden_grad, hidden_sum, mlp_out = slot(
        moves(sum_fc, "second") + back_jobs(1), mlp_work, g_both, act, slope, *fc_pieces
    )

    def rows_of(normed_t, right, *more):
        return row_grads(chips, normed_t, right, *more)

    sum_in = Scatter(chips, slot(moves(sum_fc, "near"), rows_of, normed_t, hidden_grad))
    results[2] = slot(moves(sum_in, "first") + moves(sum_fc, "far"), *attention(2))
    results[3] = slot(moves(sum_in, "second") + back_jobs(2), *attention(3))
    context = jnp.concatenate([results[group][0] for group in range(GROUPS)], axis=1)

    def out_grad(context, g_both):
        value = outer_product(context, g_both).astype(BF).reshape(count // 2, 2, d_rows, D)
        return pick(value.transpose(1, 0, 2, 3))

    out_keep, out_give = slot(
        moves(sum_in, "near") + back_jobs(3), out_grad, context, g_both
    )
    out_side, = slot(
        [core_move("out_grad", out_give)] + back_jobs(4),
        lambda mlp_out, context, out_heads: (mlp_out + dot(context, out_heads),),
        mlp_out,
        context,
        out_heads,
    )
    out_rows = jnp.concatenate(both(out_keep, box["out_grad"]), axis=0)[chips.places()]
    out_rows = (
        out_rows.reshape(count, d_rows, 2, D // 2).transpose(0, 2, 1, 3).reshape(D, D // 2)
    )

    def undo(tables, *args):
        return jnp.concatenate(
            [
                unturn(*args[3 * group : 3 * group + 3], returned(group)[1], tables)
                for group in range(GROUPS)
            ],
            axis=1,
        )

    def last_grads(tables, normed_t, out_rows, *args):
        projected_grad = undo(tables, *args)
        return projected_grad, rows_of(normed_t, projected_grad, out_rows)

    projected_grad, parts = slot(
        moves(sum_in, "far") + [core_move("out_side", out_side[row_count:])],
        last_grads,
        tables,
        normed_t,
        out_rows,
        *[
            value
            for group in range(GROUPS)
            for value in (results[group][1], results[group][2], returned(group)[0])
        ],
    )
    sum_qkv = Scatter(chips, parts)

    def input_side(projected_grad, hidden_grad, qkv_pieces, in_pieces):
        return norm_grad(projected_grad, hidden_grad, qkv_pieces, in_pieces)

    norm_part = slot(
        moves(sum_qkv, "first"), input_side, projected_grad, hidden_grad, qkv_pieces, in_pieces
    )

    def finish_output(x_own, out_side, out_more, b_rows, projected_grad):
        output = (x_own.astype(F32) + out_side + out_more + b_rows).astype(BF)
        return output, jnp.sum(projected_grad.astype(F32), axis=0)

    in_keep, in_give = pick(sum_in.result().reshape(2, d_rows, units))
    output, qkv_bias_sum = slot(
        moves(sum_qkv, "second")
        + [core_move("norm", norm_part[row_count:]), core_move("in_rows", in_give)],
        finish_output,
        x_own,
        out_side[:row_count],
        box["out_side"],
        b_rows,
        projected_grad,
    )

    def norm_back(norm_part, norm_more, xhat, inv_std, gain, g_own, chosen):
        grad = norm_part + norm_more
        xhat = xhat[:row_count]
        scaled = grad * gain
        value = (
            scaled
            - jnp.mean(scaled, axis=-1, keepdims=True)
            - xhat * jnp.mean(scaled * xhat, axis=-1, keepdims=True)
        ) * inv_std[:row_count]
        high = value.astype(BF)
        low = (value - high.astype(F32)).astype(BF)
        value = times_transposed(high, chosen) + times_transposed(low, chosen)
        sums = jnp.stack([jnp.sum(grad * xhat, axis=0), jnp.sum(grad, axis=0)])
        return (g_own.astype(F32) + value).astype(BF), sums

    input_grad, norm_sums = slot(
        moves(sum_qkv, "near"),
        norm_back,
        norm_part[:row_count],
        box["norm"],
        xhat,
        inv_std,
        gain,
        g_own,
        chosen,
    )

    norm_sums = norm_sums.reshape(2, count, 2, d_rows)[:, chips.spots()].reshape(2, D)
    mine = (jnp.arange(2) == core)[:, None]
    qkv_full = (
        jnp.where(mine, qkv_bias_sum[None, :], 0.0)
        .reshape(2, GROUPS, 3, pair, HD)
        .transpose(0, 1, 3, 2, 4)
        .reshape(3 * D)
    )
    in_full = jnp.where(
        mine[None], hidden_sum.reshape(count, 1, f_rows), 0.0
    ).reshape(2 * units)
    packed = jnp.concatenate(
        [
            vector.reshape(2 * count, -1)
            for vector in (norm_sums[0], norm_sums[1], qkv_full, grad_sum, in_full)
        ],
        axis=1,
    ).reshape(count, -1)
    order = [0]
    bits = chips.line + chips.plane
    for bit in bits:
        order = order + [chip ^ bit for chip in order]
    packed = packed[jnp.asarray(np.array(order, np.int32)) ^ chips.me]

    def fold(bit):
        return (box, "fold", packed[packed.shape[0] // 2 :], partial(chips.cross, bit=bit))

    bits = bits[::-1]
    slot(moves(sum_qkv, "far") + [fold(bits[0])])
    packed = packed[: packed.shape[0] // 2] + box["fold"]
    for bit in bits[1:]:
        half = packed.shape[0] // 2
        packed = packed[:half] + chips.cross(packed[half:], bit)
    sums_keep, sums_give = pick(packed.reshape(2, -1))
    sums = sums_keep + chips.other_core(sums_give)
    parts = []
    first = 0
    for width in (d_rows, d_rows, 3 * d_rows, d_rows, f_rows):
        parts.append(sums[first : first + width])
        first += width

    last_rows = sum_qkv.result()
    out_weight_grad = last_rows[:, qkv_wide:].reshape(2, d_rows, D // 2)
    out_weight_grad = jnp.concatenate([out_weight_grad[0], out_weight_grad[1]], axis=1)
    qkv_keep, qkv_give = pick(last_rows[:, :qkv_wide].reshape(2, d_rows, qkv_wide))
    qkv_halves = jnp.stack(both(qkv_keep, chips.other_core(qkv_give)), axis=1)
    qkv_weight_grad = (
        qkv_halves.reshape(d_rows, 2, GROUPS, 3, pair, HD)
        .transpose(0, 1, 2, 4, 3, 5)
        .reshape(d_rows, 3 * D)
    )
    in_halves = [
        value.reshape(d_rows, count, 1, f_rows) for value in both(in_keep, box["in_rows"])
    ]
    fc_in_weight_grad = jnp.concatenate(in_halves, axis=2).reshape(d_rows, 2 * units)
    return (
        output.reshape(local_seqs, tok_count, D),
        input_grad.reshape(local_seqs, tok_count, D),
        parts[0],
        parts[1],
        qkv_weight_grad,
        parts[2],
        out_weight_grad,
        parts[3],
        fc_in_weight_grad,
        parts[4],
        sum_fc.result(),
        parts[3],
    )


def solution(mesh):
    rows = P(("seq", "fsdp"))
    wide = P(("seq", "fsdp"), None)
    act = P("fsdp", "seq", None)
    placed = (act, P("fsdp", "seq"), act) + (rows, rows) + (wide, rows) * 4
    return jax.shard_map(
        local,
        mesh=mesh,
        in_specs=placed,
        out_specs=(act, act, rows, rows) + (wide, rows) * 4,
        check_vma=False,
    )
```

time: 1100 us -> 600 us (0.55)
  waiting for transfers between devices: 532 us -> 135 us
  matrix products: 195 us -> 17.2 us
  Pallas kernels: 0 us -> 174 us
  blocking collectives: 133 us -> 0 us
  starting transfers between devices: 17.6 us -> 95.8 us
  local copies, waits for them, and re-layouts: 127 us -> 87.3 us
  other arithmetic: 56.9 us -> 80.4 us
  loops' own time: 14.4 us -> 0 us
  between operations: 14.9 us -> 2.82 us
    reduce_scatter x4 -> x0, waiting for transfers between devices: 346 us -> none  [the longest x1 188 us: local(): lax.psum_scatter(fc_out_weight_grad, ('seq', 'fsdp'), scatter_dimension=0...]
    pallas_call x0 -> x19, Pallas kernels: none -> 174 us  [the longest x4 55.7 us: attend(): pl.pallas_call(partial(attend_kernel, chunks), grid=(seqs,), out_shape=(j...]
    ppermute x0 -> x60, waiting for transfers between devices: none -> 135 us  [the longest x50 93.4 us: swap(): lax.ppermute(value, axis, [(i, i ^ bit) for i in range(lax.axis_size(axis...]
    dot_general x32 -> x2, matrix products: 119 us -> 5.66 us  [dot(): return jnp.dot(left, right, preferred_element_type=F32)]
    all_to_all x4 -> x0, waiting for transfers between devices: 109 us -> none  [the longest x1 75.5 us: local(): lax.all_to_all(stacked.reshape(local_seqs, length, 1, per_group * 3 * HD)...]
    ppermute x0 -> x60, starting transfers between devices: none -> 95.8 us  [the longest x50 73.7 us: swap(): lax.ppermute(value, axis, [(i, i ^ bit) for i in range(lax.axis_size(axis...]
    unnamed x2 -> x0, blocking collectives: 83.5 us -> none
    all_gather x4 -> x0, waiting for transfers between devices: 74.3 us -> none  [the longest x1 63.6 us: local(): lax.all_gather(out_weight, ('seq', 'fsdp'), axis=0, tiled=True)]
  transfers between devices with their start and end apart: 12 -> 60, of which waited for: 7 -> 23; matrix products, arithmetic and copies ran while one was open for 32% -> 25% of each run, Pallas kernels for 0% -> 28%
where the time goes in v1:
time: 600 us; the launch traced here: 592 us
  Pallas kernels  174 us (29%)
  waiting for transfers between devices  135 us (22%)
  starting transfers between devices  95.8 us (16%)
  local copies, waits for them, and re-layouts  87.3 us (15%)
  other arithmetic  80.4 us (13%)
  matrix products  17.2 us (3%)
    ppermute x50, waiting for transfers between devices, swap(): lax.ppermute(value, axis, [(i, i ^ bit) for i in range(lax.axis_size(axis...  93.4 us
    ppermute x50, starting transfers between devices, swap(): lax.ppermute(value, axis, [(i, i ^ bit) for i in range(lax.axis_size(axis...  73.7 us
    pallas_call x4, Pallas kernels, attend(): pl.pallas_call(partial(attend_kernel, chunks), grid=(seqs,), out_shape=(j...  55.7 us
    ppermute x10, waiting for transfers between devices, shift(): lax.ppermute(value, 'seq', [(i, i + by) for i in range(count) if 0 <= i +...  41.9 us
    pallas_call x1, Pallas kernels, mlp(): pl.pallas_call(partial(mlp_kernel, chips.pieces), grid=(width // 256,), o...  22.2 us
    ppermute x10, starting transfers between devices, shift(): lax.ppermute(value, 'seq', [(i, i + by) for i in range(count) if 0 <= i +...  22.1 us
    pallas_call x2, Pallas kernels, row_grads(): pl.pallas_call(partial(row_grads_kernel, heights, steps), grid=(columns /...  19.9 us
    pallas_call x4, Pallas kernels, project(): pl.pallas_call(partial(project_kernel, len(pieces)), grid=(rows // step,)...  18 us
  transfers between devices with their start and end apart: 60, of which 23 were waited for; matrix products, arithmetic and copies ran while one was open for 25% of the time, Pallas kernels for 28%

profile of v1, /device:TPU:1, one launch (start us, length us, event | category | flops | bytes accessed | tf_op | source)
XLA Modules:
  0.0 592.4 jit_solution(1832789997073738425)
XLA Ops:
  6.5 4.5 compare_select_fusion.1
  11.3 5.8 fusion.12
  26.5 3.5 collective-permute-start.2
  30.0 4.4 fusion.27
  34.4 5.6 copy.131
  47.0 12.7 %collective-permute-done.5 = bf16[64,2560]{1,0:T(8,128)(2,1)S(1)} collective-permute-done((bf16[64,2560]{1,0:T(8,128)(2,1)S(1)}, bf16[64,2560]{1,0:T(8,128)(2,1)S(1)}, u32[]{:S(2)}, u32[]{:S(2)}) %collective-permute-start.5) | collective-permute-done | bytes 327712 | tf_op jit(solution)/shard_map/ppermute | solution.py:34
  60.7 3.1 collective-permute-start.6
  67.1 8.7 %collective-permute-done.6 = bf16[128,1024]{1,0:T(8,128)(2,1)S(1)} collective-permute-done((bf16[128,1024]{1,0:T(8,128)(2,1)}, bf16[128,1024]{1,0:T(8,128)(2,1)S(1)}, u32[]{:S(2)}, u32[]{:S(2)}) %collective-permute-start.6) | collective-permute-done | bytes 262176 | tf_op jit(solution)/shard_map/ppermute | solution.py:34
  83.6 4.2 tables.1
  89.8 8.8 %collective-permute-done.11.refs_2_ = bf16[256,1664]{1,0:T(8,128)(2,1)S(1)} collective-permute-done((bf16[256,1664]{1,0:T(8,128)(2,1)S(1)}, bf16[256,1664]{1,0:T(8,128)(2,1)S(1)}, u32[]{:S(2)}, u32[]{:S(2)}) %collective-permute-start.11) | collective-permute-done | bytes 852000 | tf_op jit(solution)/shard_map/ppermute | solution.py:34
  105.2 4.1 add_convert_fusion.normed_ref
  109.4 4.4 project.4
  120.9 4.4 project.5
  129.5 10.0 %collective-permute-done.10 = bf16[256,1024]{1,0:T(8,128)(2,1)} collective-permute-done((bf16[256,1024]{1,0:T(8,128)(2,1)}, bf16[256,1024]{1,0:T(8,128)(2,1)}, u32[]{:S(2)}, u32[]{:S(2)}) %collective-permute-start.10) | collective-permute-done | bytes 524320 | tf_op jit(solution)/shard_map/ppermute | solution.py:34
  139.6 5.2 collective-permute-done.16.refs_2_.refs_6_
  149.2 4.8 project.6
  159.6 6.5 %collective-permute-done.20.refs_2_.refs_1_ = bf16[2048,256]{1,0:T(8,128)(2,1)} collective-permute-done((bf16[2048,256]{1,0:T(8,128)(2,1)S(1)}, bf16[2048,256]{1,0:T(8,128)(2,1)}, u32[]{:S(2)}, u32[]{:S(2)}) %collective-permute-start.20) | collective-permute-done | bytes 1048608 | tf_op jit(solution)/shard_map/ppermute | solution.py:39
  169.3 4.7 collective-permute-start.22
  175.2 5.2 collective-permute-start.21
  183.7 4.4 project.7
  192.3 9.4 %collective-permute-done.21.refs_2_.refs_1_ = bf16[2048,256]{1,0:T(8,128)(2,1)} collective-permute-done((bf16[2048,256]{1,0:T(8,128)(2,1)}, bf16[2048,256]{1,0:T(8,128)(2,1)}, u32[]{:S(2)}, u32[]{:S(2)}) %collective-permute-start.21) | collective-permute-done | bytes 1048608 | tf_op jit(solution)/shard_map/ppermute | solution.py:39
  202.8 3.5 convolution_convert_fusion.1.do_ref
  206.3 4.2 collective-permute-start.23
  213.3 17.6 %hidden.1 = (bf16[1024,2048]{1,0:T(8,128)(2,1)}, bf16[2048,1024]{1,0:T(8,128)(2,1)}, f32[1024,2048]{1,0:T(8,128)}) custom-call(bf16[1024,1024]{1,0:T(8,128)(2,1)} %add_convert_fusion.normed_ref, f32[1,2048]{1,0:T(1,128)} %bitcast.220, bf16[256,2560]{1,0:T(8,128)(2,1)} %copy-done.39, bf16[256,2560]{1,0:T(8,128)(2,1)} %constant_dynamic-update-slice_fusion.4.refs_1_.refs_5_, ...), custom_call_target="tpu_custom_call" | custom-call | flops 4399824896 | bytes 18874368 | tf_op jit(solution)/shard_map/hidden/pallas_call | solution.py:416
  232.5 13.8 %attend.4 = (bf16[1024,128]{1,0:T(8,128)(2,1)}, bf16[1024,128]{1,0:T(8,128)(2,1)}, f32[1024,256]{1,0:T(8,128)}, bf16[1024,256]{1,0:T(8,128)(2,1)}, bf16[1024,256]{1,0:T(8,128)(2,1)}) custom-call(bf16[1024,128]{1,0:T(8,128)(2,1)} %get-tuple-element.322.q_ref, bf16[1024,512]{1,0:T(8,128)(2,1)} %convolution_convert_fusion.1.do_ref, ...), custom_call_target="tpu_custom_call" | custom-call | flops 2415919104 | bytes 4718592 | tf_op jit(solution)/shard_map/attend/pallas_call | solution.py:333
  247.2 10.5 %unit_grads.1 = (bf16[512,1024]{1,0:T(8,128)(2,1)}, bf16[512,1024]{1,0:T(8,128)(2,1)}, bf16[512,1024]{1,0:T(8,128)(2,1)}, bf16[512,1024]{1,0:T(8,128)(2,1)}) custom-call(s32[16]{0:T(128)} %copy-done.63, bf16[2048,1024]{1,0:T(8,128)(2,1)} %get-tuple-element.337.refs_0_.refs_1_.refs_2_.refs_3_, ...), custom_call_target="tpu_custom_call" | custom-call | flops 4294967296 | bytes 8388608 | tf_op jit(solution)/shard_map/unit_grads/pallas_call | solution.py:568
  264.9 14.0 %attend.5 = (bf16[1024,128]{1,0:T(8,128)(2,1)}, bf16[1024,128]{1,0:T(8,128)(2,1)}, f32[1024,256]{1,0:T(8,128)}, bf16[1024,256]{1,0:T(8,128)(2,1)}, bf16[1024,256]{1,0:T(8,128)(2,1)}) custom-call(bf16[1024,128]{1,0:T(8,128)(2,1)} %get-tuple-element.347.q_ref, bf16[1024,512]{1,0:T(8,128)(2,1)} %convolution_convert_fusion.1.do_ref, ...), custom_call_target="tpu_custom_call" | custom-call | flops 2415919104 | bytes 4718592 | tf_op jit(solution)/shard_map/attend/pallas_call | solution.py:333
  285.2 18.2 %collective-permute-done.27.refs_2_ = bf16[512,1024]{1,0:T(8,128)(2,1)} collective-permute-done((bf16[512,1024]{1,0:T(8,128)(2,1)}, bf16[512,1024]{1,0:T(8,128)(2,1)}, u32[]{:S(2)}, u32[]{:S(2)}) %collective-permute-start.27) | collective-permute-done | bytes 1048608 | tf_op jit(solution)/shard_map/ppermute | solution.py:34
  308.2 22.2 %mlp.1 = (bf16[1024,2048]{1,0:T(8,128)(2,1)}, f32[1,2048]{1,0:T(1,128)}, f32[1024,1024]{1,0:T(8,128)}) custom-call(s32[1]{0:T(128)} %bitcast.58.me_ref, bf16[1024,1024]{1,0:T(8,128)(2,1)} %pad_maximum_fusion.2.refs_4_.g_ref, bf16[1024,2048]{1,0:T(8,128)(2,1)} %get-tuple-element.361.act_ref, f32[1024,2048]{1,0:T(8,128)} %get-tuple-element.362.slope_ref, ...), custom_call_target="tpu_custom_call" | custom-call | flops 8589934592 | bytes 20971520 | tf_op jit(solution)/shard_map/mlp/pallas_call | solution.py:476
  339.8 10.0 %row_grads.2 = (bf16[256,2048]{1,0:T(8,128)(2,1)}, bf16[256,2048]{1,0:T(8,128)(2,1)}, bf16[256,2048]{1,0:T(8,128)(2,1)}, bf16[256,2048]{1,0:T(8,128)(2,1)}) custom-call(bf16[1024,1024]{1,0:T(8,128)(2,1)} %copy.143.left_ref, bf16[1024,2048]{1,0:T(8,128)(2,1)} %get-tuple-element.448.right_ref.hidden_ref), custom_call_target="tpu_custom_call" | custom-call | flops 4294967296 | bytes 6291456 | tf_op jit(solution)/shard_map/row_grads/pallas_call | solution.py:531
  362.2 13.8 %attend.6 = (bf16[1024,128]{1,0:T(8,128)(2,1)}, bf16[1024,128]{1,0:T(8,128)(2,1)}, f32[1024,256]{1,0:T(8,128)}, bf16[1024,256]{1,0:T(8,128)(2,1)}, bf16[1024,256]{1,0:T(8,128)(2,1)}) custom-call(bf16[1024,128]{1,0:T(8,128)(2,1)} %get-tuple-element.380.q_ref, bf16[1024,512]{1,0:T(8,128)(2,1)} %convolution_convert_fusion.1.do_ref, ...), custom_call_target="tpu_custom_call" | custom-call | flops 2415919104 | bytes 4718592 | tf_op jit(solution)/shard_map/attend/pallas_call | solution.py:333
  386.1 4.0 collective-permute-start.59
  392.0 14.0 %attend.7 = (bf16[1024,128]{1,0:T(8,128)(2,1)}, bf16[1024,128]{1,0:T(8,128)(2,1)}, f32[1024,256]{1,0:T(8,128)}, bf16[1024,256]{1,0:T(8,128)(2,1)}, bf16[1024,256]{1,0:T(8,128)(2,1)}) custom-call(bf16[1024,128]{1,0:T(8,128)(2,1)} %get-tuple-element.393.q_ref, bf16[1024,512]{1,0:T(8,128)(2,1)} %convolution_convert_fusion.1.do_ref, ...), custom_call_target="tpu_custom_call" | custom-call | flops 2415919104 | bytes 4718592 | tf_op jit(solution)/shard_map/attend/pallas_call | solution.py:333
  413.9 6.9 %collective-permute-done.39 = bf16[128,2048]{1,0:T(8,128)(2,1)S(1)} collective-permute-done((bf16[128,2048]{1,0:T(8,128)(2,1)S(1)}, bf16[128,2048]{1,0:T(8,128)(2,1)S(1)}, u32[]{:S(2)}, u32[]{:S(2)}) %collective-permute-start.39) | collective-permute-done | bytes 524320 | tf_op jit(solution)/shard_map/ppermute | solution.py:34
  422.8 17.4 %collective-permute-done.40.more_ref = bf16[2048,256]{1,0:T(8,128)(2,1)S(1)} collective-permute-done((bf16[2048,256]{1,0:T(8,128)(2,1)S(1)}, bf16[2048,256]{1,0:T(8,128)(2,1)S(1)}, u32[]{:S(2)}, u32[]{:S(2)}) %collective-permute-start.40) | collective-permute-done | bytes 1048608 | tf_op jit(solution)/shard_map/ppermute | solution.py:39
  441.2 12.2 %collective-permute-start.41 = (bf16[8,32,1024]{2,1,0:T(8,128)(2,1)S(1)}, bf16[8,32,1024]{2,1,0:T(8,128)(2,1)S(1)}, u32[]{:S(2)}, u32[]{:S(2)}) collective-permute-start(bf16[8,32,1024]{2,1,0:T(8,128)(2,1)S(1)} %fusion.5), channel_id=1, source_target_pairs={{0,1},{1,0},{2,3},{3,2},{4,5},{5,4},{6,7},{7,6},{8,9},{9,8},{10,11... | collective-permute-start | bytes 1572872 | tf_op jit(solution)/shard_map/ppermute | solution.py:34
  463.2 5.7 collective-permute-done.42.more_ref
  480.3 3.1 unturn.4
  486.3 9.8 %row_grads.3 = (bf16[256,2048]{1,0:T(8,128)(2,1)}, bf16[256,2048]{1,0:T(8,128)(2,1)}, bf16[256,2048]{1,0:T(8,128)(2,1)}, bf16[256,2048]{1,0:T(8,128)(2,1)}) custom-call(bf16[1024,1024]{1,0:T(8,128)(2,1)} %copy.151.left_ref, bf16[1024,1536]{1,0:T(8,128)(2,1)} %pad_maximum_fusion.right_ref.qkv_ref, bf16[1024,512]{1,0:T(8,128)(2,1)} %bitcast.187), custom_call_target="tpu_custom_call" | custom-call | flops 4294967296 | bytes 6291456 | tf_op jit(solution)/shard_map/row_grads/pallas_call | solution.py:531
  500.9 13.7 %norm_grad.1 = f32[1024,1024]{1,0:T(8,128)} custom-call(bf16[1024,1536]{1,0:T(8,128)(2,1)} %pad_maximum_fusion.right_ref.qkv_ref, bf16[1024,2048]{1,0:T(8,128)(2,1)} %get-tuple-element.448.right_ref.hidden_ref, bf16[256,1664]{1,0:T(8,128)(2,1)} %copy-done.5, bf16[256,1664]{1,0:T(8,128)(2,1)} %copy-done.7, bf16[256,1664]{1,0:T(8,128)(2,1)} %copy-done.8, ...), custom_call_target="tpu_custom_call" | custom-call | flops 7516192768 | bytes 12582912 | tf_op jit(solution)/shard_map/norm_grad/pallas_call | solution.py:604
  514.7 4.9 fusion.20
  531.4 3.5 add_convert_fusion.2
  535.8 6.5 %collective-permute-done.47 = bf16[128,2048]{1,0:T(8,128)(2,1)} collective-permute-done((bf16[128,2048]{1,0:T(8,128)(2,1)}, bf16[128,2048]{1,0:T(8,128)(2,1)}, u32[]{:S(2)}, u32[]{:S(2)}) %collective-permute-start.47) | collective-permute-done | bytes 524320 | tf_op jit(solution)/shard_map/ppermute | solution.py:34
  544.8 4.4 multiply_reduce_fusion.1
  550.9 6.3 %collective-permute-done.50 = bf16[128,2048]{1,0:T(8,128)(2,1)} collective-permute-done((bf16[128,2048]{1,0:T(8,128)(2,1)}, bf16[128,2048]{1,0:T(8,128)(2,1)}, u32[]{:S(2)}, u32[]{:S(2)}) %collective-permute-start.50) | collective-permute-done | bytes 524320 | tf_op jit(solution)/shard_map/ppermute | solution.py:34
  567.9 4.4 fusion.1
  573.5 5.7 collective-permute-start.55
  583.5 4.3 collective-permute-start.57
  (503 shorter events, 210.8 us)
Async XLA Ops:
  26.5 16.3 %collective-permute-start.2 = (bf16[64,1664]{1,0:T(8,128)(2,1)S(1)}, bf16[64,1664]{1,0:T(8,128)(2,1)S(1)}, u32[]{:S(2)}, u32[]{:S(2)}) collective-permute-start(bf16[64,1664]{1,0:T(8,128)(2,1)S(1)} %pad_maximum_fusion.20), channel_id=1, source_target_pairs={{0,16},{8,24},{16,0},{24,8},{1,17},{9,25},{17,1},{25,9},{2,18},{10... | collective-permute-start | bytes 638984 | tf_op jit(solution)/shard_map/ppermute | solution.py:34
  42.9 17.8 %collective-permute-start.4 = (bf16[128,1664]{1,0:T(8,128)(2,1)S(1)}, bf16[128,1664]{1,0:T(8,128)(2,1)S(1)}, u32[]{:S(2)}, u32[]{:S(2)}) collective-permute-start(bf16[128,1664]{1,0:T(8,128)(2,1)S(1)} %pad_maximum_fusion.16), channel_id=1, source_target_pairs={{0,8},{8,0},{16,24},{24,16},{1,9},{9,1},{17,25},{25,17},{2,10},{10... | collective-permute-start | bytes 1277960 | tf_op jit(solution)/shard_map/ppermute | solution.py:34
  44.2 15.5 %collective-permute-start.5 = (bf16[64,2560]{1,0:T(8,128)(2,1)S(1)}, bf16[64,2560]{1,0:T(8,128)(2,1)S(1)}, u32[]{:S(2)}, u32[]{:S(2)}) collective-permute-start(bf16[64,2560]{1,0:T(8,128)(2,1)S(1)} %maximum_maximum_fusion), channel_id=1, source_target_pairs={{0,16},{8,24},{16,0},{24,8},{1,17},{9,25},{17,1},{25,9},{2,18},{10... | collective-permute-start | bytes 983048 | tf_op jit(solution)/shard_map/ppermute | solution.py:34
  60.7 15.1 %collective-permute-start.6 = (bf16[128,1024]{1,0:T(8,128)(2,1)}, bf16[128,1024]{1,0:T(8,128)(2,1)S(1)}, u32[]{:S(2)}, u32[]{:S(2)}) collective-permute-start(bf16[128,1024]{1,0:T(8,128)(2,1)} %param.37), channel_id=1, source_target_pairs={{0,16},{8,24},{16,0},{24,8},{1,17},{9,25},{17,1},{25,9},{2,18},{10... | collective-permute-start | bytes 786440 | tf_op jit(solution)/shard_map/ppermute | solution.py:34
  63.8 12.9 %collective-permute-start.7 = (bf16[128,1664]{1,0:T(8,128)(2,1)S(1)}, bf16[128,1664]{1,0:T(8,128)(2,1)}, u32[]{:S(2)}, u32[]{:S(2)}) collective-permute-start(bf16[128,1664]{1,0:T(8,128)(2,1)S(1)} %pad_maximum_fusion.16), channel_id=1, source_target_pairs={{0,2},{1,3},{2,0},{3,1},{4,6},{5,7},{6,4},{7,5},{8,10},{9,11},{10,... | collective-permute-start | bytes 1277960 | tf_op jit(solution)/shard_map/ppermute | solution.py:34
  65.0 12.8 %collective-permute-start.8 = (bf16[128,1664]{1,0:T(8,128)(2,1)S(1)}, bf16[128,1664]{1,0:T(8,128)(2,1)}, u32[]{:S(2)}, u32[]{:S(2)}) collective-permute-start(bf16[128,1664]{1,0:T(8,128)(2,1)S(1)} %collective-permute-done.4), channel_id=1, source_target_pairs={{0,4},{1,5},{2,6},{3,7},{4,0},{5,1},{6,2},{7,3},{8,12},{9,13},{10,... | collective-permute-start | bytes 1277960 | tf_op jit(solution)/shard_map/ppermute | solution.py:34
  66.2 21.6 %collective-permute-start.9 = (bf16[128,2560]{1,0:T(8,128)(2,1)}, bf16[128,2560]{1,0:T(8,128)(2,1)}, u32[]{:S(2)}, u32[]{:S(2)}) collective-permute-start(bf16[128,2560]{1,0:T(8,128)(2,1)} %pad_maximum_fusion.14), channel_id=1, source_target_pairs={{0,8},{8,0},{16,24},{24,16},{1,9},{9,1},{17,25},{25,17},{2,10},{10... | collective-permute-start | bytes 1966088 | tf_op jit(solution)/shard_map/ppermute | solution.py:34
  79.1 19.5 %collective-permute-start.11 = (bf16[256,1664]{1,0:T(8,128)(2,1)S(1)}, bf16[256,1664]{1,0:T(8,128)(2,1)S(1)}, u32[]{:S(2)}, u32[]{:S(2)}) collective-permute-start(bf16[256,1664]{1,0:T(8,128)(2,1)S(1)} %pad_maximum_fusion.13.refs_0_), channel_id=1, source_target_pairs={{0,4},{1,5},{2,6},{3,7},{4,0},{5,1},{6,2},{7,3},{8,12},{9,13},{10,... | collective-permute-start | bytes 2555912 | tf_op jit(solution)/shard_map/ppermute | solution.py:34
  80.5 19.2 %collective-permute-start.12 = (bf16[256,1664]{1,0:T(8,128)(2,1)S(1)}, bf16[256,1664]{1,0:T(8,128)(2,1)}, u32[]{:S(2)}, u32[]{:S(2)}) collective-permute-start(bf16[256,1664]{1,0:T(8,128)(2,1)S(1)} %constant_dynamic-update-slice_fusion.2.refs_1_), channel_id=1, source_target_pairs={{0,2},{1,3},{2,0},{3,1},{4,6},{5,7},{6,4},{7,5},{8,10},{9,11},{10,... | collective-permute-start | bytes 2555912 | tf_op jit(solution)/shard_map/ppermute | solution.py:34
  99.7 14.3 %collective-permute-start.13 = (bf16[128,2560]{1,0:T(8,128)(2,1)}, bf16[128,2560]{1,0:T(8,128)(2,1)}, u32[]{:S(2)}, u32[]{:S(2)}) collective-permute-start(bf16[128,2560]{1,0:T(8,128)(2,1)} %pad_maximum_fusion.14), channel_id=1, source_target_pairs={{0,2},{1,3},{2,0},{3,1},{4,6},{5,7},{6,4},{7,5},{8,10},{9,11},{10,... | collective-permute-start | bytes 1966088 | tf_op jit(solution)/shard_map/ppermute | solution.py:34
  100.9 14.3 %collective-permute-start.14 = (bf16[128,2560]{1,0:T(8,128)(2,1)}, bf16[128,2560]{1,0:T(8,128)(2,1)}, u32[]{:S(2)}, u32[]{:S(2)}) collective-permute-start(bf16[128,2560]{1,0:T(8,128)(2,1)} %collective-permute-done.9), channel_id=1, source_target_pairs={{0,4},{1,5},{2,6},{3,7},{4,0},{5,1},{6,2},{7,3},{8,12},{9,13},{10,... | collective-permute-start | bytes 1966088 | tf_op jit(solution)/shard_map/ppermute | solution.py:34
  117.6 27.2 %collective-permute-start.16 = (bf16[256,2560]{1,0:T(8,128)(2,1)S(1)}, bf16[256,2560]{1,0:T(8,128)(2,1)}, u32[]{:S(2)}, u32[]{:S(2)}) collective-permute-start(bf16[256,2560]{1,0:T(8,128)(2,1)S(1)} %pad_maximum_fusion.3.refs_0_.refs_4_), channel_id=1, source_target_pairs={{0,4},{1,5},{2,6},{3,7},{4,0},{5,1},{6,2},{7,3},{8,12},{9,13},{10,... | collective-permute-start | bytes 3932168 | tf_op jit(solution)/shard_map/ppermute | solution.py:34
  118.7 27.5 %collective-permute-start.17 = (bf16[256,2560]{1,0:T(8,128)(2,1)}, bf16[256,2560]{1,0:T(8,128)(2,1)}, u32[]{:S(2)}, u32[]{:S(2)}) collective-permute-start(bf16[256,2560]{1,0:T(8,128)(2,1)} %constant_dynamic-update-slice_fusion.4.refs_1_.refs_5_), channel_id=1, source_target_pairs={{0,2},{1,3},{2,0},{3,1},{4,6},{5,7},{6,4},{7,5},{8,10},{9,11},{10,... | collective-permute-start | bytes 3932168 | tf_op jit(solution)/shard_map/ppermute | solution.py:34
  120.5 19.1 %collective-permute-start.10 = (bf16[256,1024]{1,0:T(8,128)(2,1)}, bf16[256,1024]{1,0:T(8,128)(2,1)}, u32[]{:S(2)}, u32[]{:S(2)}) collective-permute-start(bf16[256,1024]{1,0:T(8,128)(2,1)} %get-tuple-element.311), channel_id=1, source_target_pairs={{0,8},{8,0},{16,24},{24,16},{1,9},{9,1},{17,25},{25,17},{2,10},{10... | collective-permute-start | bytes 1572872 | tf_op jit(solution)/shard_map/ppermute | solution.py:34
  146.2 20.0 %collective-permute-start.20 = (bf16[2048,256]{1,0:T(8,128)(2,1)S(1)}, bf16[2048,256]{1,0:T(8,128)(2,1)}, u32[]{:S(2)}, u32[]{:S(2)}) collective-permute-start(bf16[2048,256]{1,0:T(8,128)(2,1)S(1)} %pad_maximum_fusion.5), channel_id=1, source_target_pairs={{0,8},{8,16},{16,24},{1,9},{9,17},{17,25},{2,10},{10,18},{18,26},{... | collective-permute-start | bytes 3145736 | tf_op jit(solution)/shard_map/ppermute | solution.py:39
  169.3 22.6 %collective-permute-start.22 = (bf16[16,32,1024]{2,1,0:T(8,128)(2,1)S(1)}, bf16[16,32,1024]{2,1,0:T(8,128)(2,1)S(1)}, u32[]{:S(2)}, u32[]{:S(2)}) collective-permute-start(bf16[16,32,1024]{2,1,0:T(8,128)(2,1)S(1)} %gather_fusion.4), channel_id=1, source_target_pairs={{0,1},{1,0},{2,3},{3,2},{4,5},{5,4},{6,7},{7,6},{8,9},{9,8},{10,11... | collective-permute-start | bytes 3145736 | tf_op jit(solution)/shard_map/ppermute | solution.py:34
  174.0 14.1 %collective-permute-start.18 = (bf16[256,1024]{1,0:T(8,128)(2,1)}, bf16[256,1024]{1,0:T(8,128)(2,1)}, u32[]{:S(2)}, u32[]{:S(2)}) collective-permute-start(bf16[256,1024]{1,0:T(8,128)(2,1)} %get-tuple-element.311), channel_id=1, source_target_pairs={{0,2},{1,3},{2,0},{3,1},{4,6},{5,7},{6,4},{7,5},{8,10},{9,11},{10,... | collective-permute-start | bytes 1572872 | tf_op jit(solution)/shard_map/ppermute | solution.py:34
  174.1 15.8 %collective-permute-start.19 = (bf16[256,1024]{1,0:T(8,128)(2,1)}, bf16[256,1024]{1,0:T(8,128)(2,1)}, u32[]{:S(2)}, u32[]{:S(2)}) collective-permute-start(bf16[256,1024]{1,0:T(8,128)(2,1)} %collective-permute-done.10), channel_id=1, source_target_pairs={{0,4},{1,5},{2,6},{3,7},{4,0},{5,1},{6,2},{7,3},{8,12},{9,13},{10,... | collective-permute-start | bytes 1572872 | tf_op jit(solution)/shard_map/ppermute | solution.py:34
  175.2 26.5 %collective-permute-start.21 = (bf16[2048,256]{1,0:T(8,128)(2,1)}, bf16[2048,256]{1,0:T(8,128)(2,1)}, u32[]{:S(2)}, u32[]{:S(2)}) collective-permute-start(bf16[2048,256]{1,0:T(8,128)(2,1)} %pad_maximum_fusion.7), channel_id=1, source_target_pairs={{0,8},{8,16},{16,24},{1,9},{9,17},{17,25},{2,10},{10,18},{18,26},{... | collective-permute-start | bytes 3145736 | tf_op jit(solution)/shard_map/ppermute | solution.py:39
  180.4 22.4 %collective-permute-start.3 = (bf16[512,1024]{1,0:T(8,128)(2,1)S(1)}, bf16[512,1024]{1,0:T(8,128)(2,1)}, u32[]{:S(2)}, u32[]{:S(2)}) collective-permute-start(bf16[512,1024]{1,0:T(8,128)(2,1)S(1)} %bitcast.177), channel_id=1, source_target_pairs={{0,1},{1,0},{2,3},{3,2},{4,5},{5,4},{6,7},{7,6},{8,9},{9,8},{10,11... | collective-permute-start | bytes 3145736 | tf_op jit(solution)/shard_map/ppermute | solution.py:34
  206.3 40.0 %collective-permute-start.23 = (bf16[2048,256]{1,0:T(8,128)(2,1)S(1)}, bf16[2048,256]{1,0:T(8,128)(2,1)S(1)}, u32[]{:S(2)}, u32[]{:S(2)}) collective-permute-start(bf16[2048,256]{1,0:T(8,128)(2,1)S(1)} %pad_maximum_fusion.8), channel_id=1, source_target_pairs={{0,8},{8,16},{16,24},{1,9},{9,17},{17,25},{2,10},{10,18},{18,26},{... | collective-permute-start | bytes 3145736 | tf_op jit(solution)/shard_map/ppermute | solution.py:39
  257.7 23.6 %collective-permute-start.25 = (bf16[512,1024]{1,0:T(8,128)(2,1)}, bf16[512,1024]{1,0:T(8,128)(2,1)S(1)}, u32[]{:S(2)}, u32[]{:S(2)}) collective-permute-start(bf16[512,1024]{1,0:T(8,128)(2,1)} %get-tuple-element.344), channel_id=1, source_target_pairs={{0,4},{1,5},{2,6},{3,7},{4,0},{5,1},{6,2},{7,3},{8,12},{9,13},{10,... | collective-permute-start | bytes 3145736 | tf_op jit(solution)/shard_map/ppermute | solution.py:34
  258.1 20.8 %collective-permute-start.26 = (bf16[1024,256]{1,0:T(8,128)(2,1)}, bf16[1024,256]{1,0:T(8,128)(2,1)S(1)}, u32[]{:S(2)}, u32[]{:S(2)}) collective-permute-start(bf16[1024,256]{1,0:T(8,128)(2,1)} %get-tuple-element.346), channel_id=1, source_target_pairs={{8,0},{16,8},{24,16},{9,1},{17,9},{25,17},{10,2},{18,10},{26,18},{... | collective-permute-start | bytes 1572872 | tf_op jit(solution)/shard_map/ppermute | solution.py:39
  260.0 22.9 %collective-permute-start.24 = (bf16[512,1024]{1,0:T(8,128)(2,1)}, bf16[512,1024]{1,0:T(8,128)(2,1)S(1)}, u32[]{:S(2)}, u32[]{:S(2)}) collective-permute-start(bf16[512,1024]{1,0:T(8,128)(2,1)} %get-tuple-element.342), channel_id=1, source_target_pairs={{0,2},{1,3},{2,0},{3,1},{4,6},{5,7},{6,4},{7,5},{8,10},{9,11},{10,... | collective-permute-start | bytes 3145736 | tf_op jit(solution)/shard_map/ppermute | solution.py:34
  262.0 41.4 %collective-permute-start.27 = (bf16[512,1024]{1,0:T(8,128)(2,1)}, bf16[512,1024]{1,0:T(8,128)(2,1)}, u32[]{:S(2)}, u32[]{:S(2)}) collective-permute-start(bf16[512,1024]{1,0:T(8,128)(2,1)} %constant_dynamic-update-slice_fusion.6.refs_0_), channel_id=1, source_target_pairs={{0,4},{1,5},{2,6},{3,7},{4,0},{5,1},{6,2},{7,3},{8,12},{9,13},{10,... | collective-permute-start | bytes 3145736 | tf_op jit(solution)/shard_map/ppermute | solution.py:34
  262.1 43.4 %collective-permute-start.28 = (bf16[512,1024]{1,0:T(8,128)(2,1)}, bf16[512,1024]{1,0:T(8,128)(2,1)}, u32[]{:S(2)}, u32[]{:S(2)}) collective-permute-start(bf16[512,1024]{1,0:T(8,128)(2,1)} %constant_dynamic-update-slice_fusion.9.refs_1_), channel_id=1, source_target_pairs={{0,2},{1,3},{2,0},{3,1},{4,6},{5,7},{6,4},{7,5},{8,10},{9,11},{10,... | collective-permute-start | bytes 3145736 | tf_op jit(solution)/shard_map/ppermute | solution.py:34
  305.5 24.9 %collective-permute-start.29 = (bf16[256,1024]{1,0:T(8,128)(2,1)}, bf16[256,1024]{1,0:T(8,128)(2,1)}, u32[]{:S(2)}, u32[]{:S(2)}) collective-permute-start(bf16[256,1024]{1,0:T(8,128)(2,1)} %slice.485), channel_id=1, source_target_pairs={{0,4},{1,5},{2,6},{3,7},{4,0},{5,1},{6,2},{7,3},{8,12},{9,13},{10,... | collective-permute-start | bytes 1572872 | tf_op jit(solution)/shard_map/ppermute | solution.py:34
  306.6 43.3 %collective-permute-start.30 = (bf16[256,1024]{1,0:T(8,128)(2,1)}, bf16[256,1024]{1,0:T(8,128)(2,1)}, u32[]{:S(2)}, u32[]{:S(2)}) collective-permute-start(bf16[256,1024]{1,0:T(8,128)(2,1)} %slice.484), channel_id=1, source_target_pairs={{0,2},{1,3},{2,0},{3,1},{4,6},{5,7},{6,4},{7,5},{8,10},{9,11},{10,... | collective-permute-start | bytes 1572872 | tf_op jit(solution)/shard_map/ppermute | solution.py:34
  306.9 51.5 %collective-permute-start.34 = (bf16[2048,256]{1,0:T(8,128)(2,1)}, bf16[2048,256]{1,0:T(8,128)(2,1)}, u32[]{:S(2)}, u32[]{:S(2)}) collective-permute-start(bf16[2048,256]{1,0:T(8,128)(2,1)} %pad_maximum_fusion.9), channel_id=1, source_target_pairs={{8,0},{16,8},{24,16},{9,1},{17,9},{25,17},{10,2},{18,10},{26,18},{... | collective-permute-start | bytes 3145736 | tf_op jit(solution)/shard_map/ppermute | solution.py:39
  332.8 17.1 %collective-permute-start.31 = (bf16[256,1024]{1,0:T(8,128)(2,1)}, bf16[256,1024]{1,0:T(8,128)(2,1)}, u32[]{:S(2)}, u32[]{:S(2)}) collective-permute-start(bf16[256,1024]{1,0:T(8,128)(2,1)} %add_convert_fusion.14), channel_id=1, source_target_pairs={{0,8},{8,0},{16,24},{24,16},{1,9},{9,1},{17,25},{25,17},{2,10},{10... | collective-permute-start | bytes 1572872 | tf_op jit(solution)/shard_map/ppermute | solution.py:34
  353.0 25.3 %collective-permute-start.32 = (bf16[256,2048]{1,0:T(8,128)(2,1)}, bf16[256,2048]{1,0:T(8,128)(2,1)}, u32[]{:S(2)}, u32[]{:S(2)}) collective-permute-start(bf16[256,2048]{1,0:T(8,128)(2,1)} %get-tuple-element.375), channel_id=1, source_target_pairs={{0,4},{1,5},{2,6},{3,7},{4,0},{5,1},{6,2},{7,3},{8,12},{9,13},{10,... | collective-permute-start | bytes 3145736 | tf_op jit(solution)/shard_map/ppermute | solution.py:34
  355.5 28.1 %collective-permute-start.35 = (bf16[1024,256]{1,0:T(8,128)(2,1)}, bf16[1024,256]{1,0:T(8,128)(2,1)}, u32[]{:S(2)}, u32[]{:S(2)}) collective-permute-start(bf16[1024,256]{1,0:T(8,128)(2,1)} %slice.482), channel_id=1, source_target_pairs={{0,8},{8,16},{16,24},{1,9},{9,17},{17,25},{2,10},{10,18},{18,26},{... | collective-permute-start | bytes 1572872 | tf_op jit(solution)/shard_map/ppermute | solution.py:39
  358.2 22.8 %collective-permute-start.33 = (bf16[256,2048]{1,0:T(8,128)(2,1)}, bf16[256,2048]{1,0:T(8,128)(2,1)}, u32[]{:S(2)}, u32[]{:S(2)}) collective-permute-start(bf16[256,2048]{1,0:T(8,128)(2,1)} %get-tuple-element.377), channel_id=1, source_target_pairs={{0,2},{1,3},{2,0},{3,1},{4,6},{5,7},{6,4},{7,5},{8,10},{9,11},{10,... | collective-permute-start | bytes 3145736 | tf_op jit(solution)/shard_map/ppermute | solution.py:34
  383.6 23.6 %collective-permute-start.37 = (bf16[128,2048]{1,0:T(8,128)(2,1)}, bf16[128,2048]{1,0:T(8,128)(2,1)}, u32[]{:S(2)}, u32[]{:S(2)}) collective-permute-start(bf16[128,2048]{1,0:T(8,128)(2,1)} %slice.490), channel_id=1, source_target_pairs={{0,4},{1,5},{2,6},{3,7},{4,0},{5,1},{6,2},{7,3},{8,12},{9,13},{10,... | collective-permute-start | bytes 1572872 | tf_op jit(solution)/shard_map/ppermute | solution.py:34
  384.7 23.9 %collective-permute-start.38 = (bf16[2048,256]{1,0:T(8,128)(2,1)}, bf16[2048,256]{1,0:T(8,128)(2,1)}, u32[]{:S(2)}, u32[]{:S(2)}) collective-permute-start(bf16[2048,256]{1,0:T(8,128)(2,1)} %pad_maximum_fusion.10), channel_id=1, source_target_pairs={{8,0},{16,8},{24,16},{9,1},{17,9},{25,17},{10,2},{18,10},{26,18},{... | collective-permute-start | bytes 3145736 | tf_op jit(solution)/shard_map/ppermute | solution.py:39
  386.1 141.4 %collective-permute-start.59 = (bf16[128,1024]{1,0:T(8,128)(2,1)}, bf16[128,1024]{1,0:T(8,128)(2,1)S(1)}, u32[]{:S(2)}, u32[]{:S(2)}) collective-permute-start(bf16[128,1024]{1,0:T(8,128)(2,1)} %slice.630), channel_id=1, source_target_pairs={{0,16},{8,24},{16,0},{24,8},{1,17},{9,25},{17,1},{25,9},{2,18},{10... | collective-permute-start | bytes 786440 | tf_op jit(solution)/shard_map/ppermute | solution.py:34
  391.8 22.1 %collective-permute-start.36 = (bf16[128,2048]{1,0:T(8,128)(2,1)}, bf16[128,2048]{1,0:T(8,128)(2,1)}, u32[]{:S(2)}, u32[]{:S(2)}) collective-permute-start(bf16[128,2048]{1,0:T(8,128)(2,1)} %slice.489), channel_id=1, source_target_pairs={{0,2},{1,3},{2,0},{3,1},{4,6},{5,7},{6,4},{7,5},{8,10},{9,11},{10,... | collective-permute-start | bytes 1572872 | tf_op jit(solution)/shard_map/ppermute | solution.py:34
  411.2 29.0 %collective-permute-start.40 = (bf16[2048,256]{1,0:T(8,128)(2,1)S(1)}, bf16[2048,256]{1,0:T(8,128)(2,1)S(1)}, u32[]{:S(2)}, u32[]{:S(2)}) collective-permute-start(bf16[2048,256]{1,0:T(8,128)(2,1)S(1)} %pad_maximum_fusion.11), channel_id=1, source_target_pairs={{8,0},{16,8},{24,16},{9,1},{17,9},{25,17},{10,2},{18,10},{26,18},{... | collective-permute-start | bytes 3145736 | tf_op jit(solution)/shard_map/ppermute | solution.py:39
  441.2 17.0 %collective-permute-start.41 = (bf16[8,32,1024]{2,1,0:T(8,128)(2,1)S(1)}, bf16[8,32,1024]{2,1,0:T(8,128)(2,1)S(1)}, u32[]{:S(2)}, u32[]{:S(2)}) collective-permute-start(bf16[8,32,1024]{2,1,0:T(8,128)(2,1)S(1)} %fusion.5), channel_id=1, source_target_pairs={{0,1},{1,0},{2,3},{3,2},{4,5},{5,4},{6,7},{7,6},{8,9},{9,8},{10,11... | collective-permute-start | bytes 1572872 | tf_op jit(solution)/shard_map/ppermute | solution.py:34
  453.4 15.6 %collective-permute-start.42 = (bf16[1024,256]{1,0:T(8,128)(2,1)}, bf16[1024,256]{1,0:T(8,128)(2,1)}, u32[]{:S(2)}, u32[]{:S(2)}) collective-permute-start(bf16[1024,256]{1,0:T(8,128)(2,1)} %add_convert_fusion.10), channel_id=1, source_target_pairs={{8,0},{16,8},{24,16},{9,1},{17,9},{25,17},{10,2},{18,10},{26,18},{... | collective-permute-start | bytes 1572872 | tf_op jit(solution)/shard_map/ppermute | solution.py:39
  496.1 24.2 %collective-permute-start.43 = (bf16[256,2048]{1,0:T(8,128)(2,1)}, bf16[256,2048]{1,0:T(8,128)(2,1)}, u32[]{:S(2)}, u32[]{:S(2)}) collective-permute-start(bf16[256,2048]{1,0:T(8,128)(2,1)} %get-tuple-element.444), channel_id=1, source_target_pairs={{0,4},{1,5},{2,6},{3,7},{4,0},{5,1},{6,2},{7,3},{8,12},{9,13},{10,... | collective-permute-start | bytes 3145736 | tf_op jit(solution)/shard_map/ppermute | solution.py:34
  496.5 25.9 %collective-permute-start.44 = (bf16[256,2048]{1,0:T(8,128)(2,1)}, bf16[256,2048]{1,0:T(8,128)(2,1)}, u32[]{:S(2)}, u32[]{:S(2)}) collective-permute-start(bf16[256,2048]{1,0:T(8,128)(2,1)} %get-tuple-element.446), channel_id=1, source_target_pairs={{0,2},{1,3},{2,0},{3,1},{4,6},{5,7},{6,4},{7,5},{8,10},{9,11},{10,... | collective-permute-start | bytes 3145736 | tf_op jit(solution)/shard_map/ppermute | solution.py:34
  497.8 21.7 %collective-permute-start.45 = (bf16[64,2048]{1,0:T(8,128)(2,1)S(1)}, bf16[64,2048]{1,0:T(8,128)(2,1)S(1)}, u32[]{:S(2)}, u32[]{:S(2)}) collective-permute-start(bf16[64,2048]{1,0:T(8,128)(2,1)S(1)} %copy-done.61), channel_id=1, source_target_pairs={{0,16},{8,24},{16,0},{24,8},{1,17},{9,25},{17,1},{25,9},{2,18},{10... | collective-permute-start | bytes 786440 | tf_op jit(solution)/shard_map/ppermute | solution.py:34
  499.1 27.1 %collective-permute-start.46 = (f32[512,1024]{1,0:T(8,128)S(1)}, f32[512,1024]{1,0:T(8,128)}, u32[]{:S(2)}, u32[]{:S(2)}) collective-permute-start(f32[512,1024]{1,0:T(8,128)S(1)} %copy-done.38), channel_id=1, source_target_pairs={{0,1},{1,0},{2,3},{3,2},{4,5},{5,4},{6,7},{7,6},{8,9},{9,8},{10,11... | collective-permute-start | bytes 6291464 | tf_op jit(solution)/shard_map/ppermute | solution.py:34
  526.2 18.0 %collective-permute-start.48 = (f32[512,1024]{1,0:T(8,128)}, f32[512,1024]{1,0:T(8,128)}, u32[]{:S(2)}, u32[]{:S(2)}) collective-permute-start(f32[512,1024]{1,0:T(8,128)} %get-tuple-element.464), channel_id=1, source_target_pairs={{0,1},{1,0},{2,3},{3,2},{4,5},{5,4},{6,7},{7,6},{8,9},{9,8},{10,11... | collective-permute-start | bytes 6291464 | tf_op jit(solution)/shard_map/ppermute | solution.py:34
  528.4 13.9 %collective-permute-start.47 = (bf16[128,2048]{1,0:T(8,128)(2,1)}, bf16[128,2048]{1,0:T(8,128)(2,1)}, u32[]{:S(2)}, u32[]{:S(2)}) collective-permute-start(bf16[128,2048]{1,0:T(8,128)(2,1)} %slice.500), channel_id=1, source_target_pairs={{0,4},{1,5},{2,6},{3,7},{4,0},{5,1},{6,2},{7,3},{8,12},{9,13},{10,... | collective-permute-start | bytes 1572872 | tf_op jit(solution)/shard_map/ppermute | solution.py:34
  528.8 22.2 %collective-permute-start.49 = (bf16[128,2048]{1,0:T(8,128)(2,1)}, bf16[128,2048]{1,0:T(8,128)(2,1)}, u32[]{:S(2)}, u32[]{:S(2)}) collective-permute-start(bf16[128,2048]{1,0:T(8,128)(2,1)} %slice.499), channel_id=1, source_target_pairs={{0,2},{1,3},{2,0},{3,1},{4,6},{5,7},{6,4},{7,5},{8,10},{9,11},{10,... | collective-permute-start | bytes 1572872 | tf_op jit(solution)/shard_map/ppermute | solution.py:34
  544.2 13.0 %collective-permute-start.50 = (bf16[128,2048]{1,0:T(8,128)(2,1)}, bf16[128,2048]{1,0:T(8,128)(2,1)}, u32[]{:S(2)}, u32[]{:S(2)}) collective-permute-start(bf16[128,2048]{1,0:T(8,128)(2,1)} %add_convert_fusion.9), channel_id=1, source_target_pairs={{0,8},{8,0},{16,24},{24,16},{1,9},{9,1},{17,25},{25,17},{2,10},{10... | collective-permute-start | bytes 1572872 | tf_op jit(solution)/shard_map/ppermute | solution.py:34
  (99 other events, 969.5 us)
